TPU v7x, 1024 devices: a whole 4x8x16 slice. The times are simulated.
1024 devices in a mesh: fsdp: 32 (over x, z_hi, core), expert: 32 (over z_lo, y).
Axes of the slice: x: 4, y: 8, z: 16 (z_hi: 4, z_lo: 4; z = z_hi * 4 + z_lo), core: 2. Of those that a mesh axis runs over, the one named last changes fastest.
Arguments:
- tokens: bfloat16 [256, 6144], P('expert', 'fsdp'), may hold values from -6 to 6
- cotangent: bfloat16 [256, 6144], P('expert', 'fsdp'), may hold values from -6 to 6
- routes: int32 [256, 2], P('expert'), may hold values from 0 to 3, all different within a row; in each aligned block of 8 rows (0 to 7, 8 to 15, ...) at most 8 rows name the same one
- route_weights: float32 [256, 2], P('expert'), may hold values from 0.1 to 0.9
- domains: int32 [256], P('expert'), may hold values from 0 to 7
- loss_weights: float32 [8], replicated, may hold values from 0.25 to 4
- w_gate: bfloat16 [32, 6144, 1536], P('expert', 'fsdp'), may hold values from -0.078125 to 0.078125
- w_up: bfloat16 [32, 6144, 1536], P('expert', 'fsdp'), may hold values from -0.078125 to 0.078125
- w_down: bfloat16 [32, 1536, 6144], P('expert', None, 'fsdp'), may hold values from -0.0546875 to 0.0546875
Outputs:
- mixed: bfloat16 [256, 6144], P('expert', 'fsdp')
- grad_tokens: bfloat16 [256, 6144], P('expert', 'fsdp')
- grad_gate: bfloat16 [32, 6144, 1536], P('expert', 'fsdp')
- grad_up: bfloat16 [32, 6144, 1536], P('expert', 'fsdp')
- grad_down: bfloat16 [32, 1536, 6144], P('expert', None, 'fsdp')
Inputs may be any that keep to these rules, and one draw needn't show every extreme that they name: `routes`: each row names 2 different experts. Within the rows of one index of expert (aligned blocks of 8 rows) no expert is named more than 8 times, and in every draw some block names some expert exactly 8 times.
All inputs are finite; a program needn't handle non-finite values.
Results may differ from a plain program's by a relative error of at most 0.014.
Values may be sent and summed in bfloat16 or wider, within the bound.
No kernel may reach another device: no remote copies, remote signals or barrier semaphores. Data moves between devices by JAX's collectives and lax.ppermute only.
A program may use at most 32 MiB of HBM per device.

v0:
```python
import jax
import jax.numpy as jnp
from jax import lax
from jax.sharding import PartitionSpec as P

EXPERTS = 4
DOMAINS = 8


def send_rows(buffer):
    return lax.all_to_all(buffer, "expert", split_axis=0, concat_axis=0, tiled=True)


def return_rows(buffer):
    return lax.all_to_all(buffer, "expert", split_axis=0, concat_axis=0, tiled=True)


def per_device(
    tokens, cotangent, routes, route_weights, domains, loss_weights, w_gate, w_up, w_down
):
    tok_count, local_width = tokens.shape
    dev_expert = lax.axis_size("expert")
    dev_fsdp = lax.axis_size("fsdp")
    groups = dev_expert // EXPERTS
    grp_width = w_gate.shape[2]
    share = grp_width // dev_fsdp
    slots = dev_expert * tok_count
    pairs = 2 * tok_count
    picks = routes.reshape(-1)
    onehot = (picks[:, None] == jnp.arange(EXPERTS, dtype=jnp.int32)[None, :]).astype(jnp.int32)
    before = jnp.cumsum(onehot, axis=0) - onehot
    places = jnp.sum(before * onehot, axis=1)
    owners = (jnp.arange(dev_expert, dtype=jnp.int32) // groups)[:, None, None]
    spots = jnp.arange(tok_count, dtype=jnp.int32)[None, :, None]
    assign = ((picks[None, None, :] == owners) & (places[None, None, :] == spots)).reshape(
        slots, pairs
    )
    assign_low = assign.astype(jnp.bfloat16)
    assign_high = assign.astype(jnp.float32)
    domain_hit = domains[:, None] == jnp.arange(DOMAINS, dtype=jnp.int32)[None, :]
    token_scale = jnp.sum(jnp.where(domain_hit, loss_weights[None, :], jnp.float32(0.0)), axis=1)
    scaled = (cotangent.astype(jnp.float32) * token_scale[:, None]).astype(jnp.bfloat16)
    tok_pairs = jnp.repeat(tokens, 2, axis=0)
    grad_pairs = (
        route_weights.reshape(-1)[:, None] * jnp.repeat(scaled, 2, axis=0).astype(jnp.float32)
    ).astype(jnp.bfloat16)
    sent_tokens = jnp.dot(assign_low, tok_pairs, preferred_element_type=jnp.float32).astype(
        jnp.bfloat16
    )
    sent_tokens = sent_tokens.reshape(dev_expert, tok_count, local_width)
    sent_grads = jnp.dot(assign_low, grad_pairs, preferred_element_type=jnp.float32).astype(
        jnp.bfloat16
    )
    sent_grads = sent_grads.reshape(dev_expert, tok_count, local_width)
    tok_rows = send_rows(sent_tokens)
    x_rows = tok_rows.reshape(slots, local_width)
    gate_local = w_gate[0]
    up_local = w_up[0]
    down_local = w_down[0]
    blocks = lax.axis_size("fsdp") * (2 * share) // (2 * share)
    gate_cols = gate_local
    up_cols = up_local
    gate_part = jnp.einsum("dc,rd->cr", gate_cols, x_rows, preferred_element_type=jnp.float32)
    up_part = jnp.einsum("dc,rd->cr", up_cols, x_rows, preferred_element_type=jnp.float32)
    joined = jnp.stack(
        [gate_part.reshape(blocks, share, slots), up_part.reshape(blocks, share, slots)], axis=1
    )
    shares = lax.psum_scatter(
        joined.reshape(lax.axis_size("fsdp") * (2 * share), slots),
        "fsdp",
        scatter_dimension=0,
        tiled=True,
    )
    gate_share = shares[:share]
    up_share = shares[share:]
    sigma = jax.nn.sigmoid(gate_share)
    hidden = (gate_share * sigma * up_share).astype(jnp.bfloat16)
    piece = lax.all_gather(hidden, "fsdp", axis=0, tiled=True)
    down_rows = down_local
    total = jnp.einsum("nr,nd->rd", piece, down_rows, preferred_element_type=jnp.float32)
    out_part = total
    out_block = out_part.reshape(dev_expert, tok_count, local_width)
    out_back = return_rows(out_block)
    grad_rows = send_rows(sent_grads)
    de_rows = grad_rows.reshape(slots, local_width)
    down_rows = down_local
    hidden_grad = lax.psum_scatter(
        jnp.einsum("cd,rd->cr", down_rows, de_rows, preferred_element_type=jnp.float32),
        "fsdp",
        scatter_dimension=0,
        tiled=True,
    )
    gate_grad = (hidden_grad * up_share * sigma * (1.0 + gate_share * (1.0 - sigma))).astype(
        jnp.bfloat16
    )
    up_grad = (hidden_grad * gate_share * sigma).astype(jnp.bfloat16)
    gate_piece = lax.all_gather(gate_grad, "fsdp", axis=0, tiled=True)
    up_piece = lax.all_gather(up_grad, "fsdp", axis=0, tiled=True)
    gate_cols = gate_local
    up_cols = up_local
    total = jnp.einsum("nr,dn->rd", gate_piece, gate_cols, preferred_element_type=jnp.float32)
    total = total + jnp.einsum("nr,dn->rd", up_piece, up_cols, preferred_element_type=jnp.float32)
    gate_new = jnp.einsum("rd,nr->dn", x_rows, gate_piece, preferred_element_type=jnp.float32)
    up_new = jnp.einsum("rd,nr->dn", x_rows, up_piece, preferred_element_type=jnp.float32)
    gate_acc = gate_new
    up_acc = up_new
    input_part, gate_acc, up_acc = (total, gate_acc, up_acc)
    down_acc = jnp.dot(piece, de_rows, preferred_element_type=jnp.float32)
    input_block = input_part.reshape(dev_expert, tok_count, local_width)
    input_back = return_rows(input_block)
    out_pairs = jnp.dot(
        assign_high.T, out_back.reshape(slots, local_width), precision=lax.Precision.HIGHEST
    )
    input_pairs = jnp.dot(
        assign_high.T, input_back.reshape(slots, local_width), precision=lax.Precision.HIGHEST
    )
    mixed = jnp.sum(
        route_weights[:, :, None] * out_pairs.reshape(tok_count, 2, local_width), axis=1
    )
    grad_tokens = jnp.sum(input_pairs.reshape(tok_count, 2, local_width), axis=1)
    return (
        mixed.astype(jnp.bfloat16),
        grad_tokens.astype(jnp.bfloat16),
        gate_acc.astype(jnp.bfloat16)[None],
        up_acc.astype(jnp.bfloat16)[None],
        down_acc.astype(jnp.bfloat16)[None],
    )


def solution(mesh):
    in_specs = (
        P("expert", "fsdp"),
        P("expert", "fsdp"),
        P("expert", None),
        P("expert", None),
        P("expert"),
        P(),
        P("expert", "fsdp", None),
        P("expert", "fsdp", None),
        P("expert", None, "fsdp"),
    )
    out_specs = (
        P("expert", "fsdp"),
        P("expert", "fsdp"),
        P("expert", "fsdp", None),
        P("expert", "fsdp", None),
        P("expert", None, "fsdp"),
    )
    return jax.shard_map(
        per_device, mesh=mesh, in_specs=in_specs, out_specs=out_specs, check_vma=False
    )
```

profile of v0, /device:TPU:8, one launch (start us, length us, event | category | flops | bytes accessed | tf_op | source)
XLA Modules:
  0.0 512.3 jit_solution(383844606571748828)
XLA Ops:
  7.2 0.0 copy-start
  7.2 0.0 reduce-scatter.9.cloned.1.call-start
  7.2 0.8 copy.80
  8.0 0.1 eq.64
  8.1 0.1 fusion.25
  8.2 0.2 select_reduce_fusion
  8.4 0.1 broadcast_compare_fusion
  8.5 0.9 select_reduce_fusion.1
  9.4 0.8 fusion.28
  10.1 0.7 multiply_convert_fusion.3
  10.9 0.2 convolution_convert_fusion.3
  11.2 0.1 copy.93
  11.3 25.5 %all_to_all.20 = bf16[32,8,192]{2,1,0:T(8,128)(2,1)S(1)} all-to-all(bf16[32,8,192]{2,1,0:T(8,128)(2,1)S(1)} %bitcast.82), channel_id=1, replica_groups=mesh['fsdp'=32,'expert'=32] {'expert'}, dimensions={0} | all-to-all | bytes 196608 | tf_op jit(solution)/shard_map/all_to_all | solution.py:11
  36.8 1.4 convolution_bitcast_fusion
  38.2 1.6 copy.105
  39.8 0.0 reduce-scatter.9.cloned.1.call-update
  39.8 0.0 reduce-scatter.7.cloned.1.call-start
  39.9 0.6 copy-done.3
  40.5 0.2 convolution_convert_fusion.4
  40.7 0.1 copy.82
  40.9 13.5 %all_to_all.21 = bf16[32,8,192]{2,1,0:T(8,128)(2,1)S(1)} all-to-all(bf16[32,8,192]{2,1,0:T(8,128)(2,1)S(1)} %bitcast.83), channel_id=1, replica_groups=mesh['fsdp'=32,'expert'=32] {'expert'}, dimensions={0} | all-to-all | bytes 196608 | tf_op jit(solution)/shard_map/all_to_all | solution.py:11
  54.4 0.4 convolution_bitcast_fusion.2
  54.8 1.6 copy.83
  56.4 0.4 convolution_bitcast_fusion.1
  56.8 1.6 copy.84
  58.4 2.1 pad_maximum_fusion
  60.5 2.0 copy.85
  62.5 0.0 reduce-scatter.7.cloned.1.call-update
  62.5 103.7 %reduce-scatter.9.cloned.1.call-done = f32[48,256]{1,0:T(8,128)} async-done(((f32[1536,256]{1,0:T(8,128)}), f32[48,256]{1,0:T(8,128)}) %reduce-scatter.9.cloned.1.call-update) | async-done | bytes 49168 | tf_op jit(solution)/shard_map/reduce_scatter | solution.py:87
  166.2 140.1 %reduce-scatter.7.cloned.1.call-done = f32[96,256]{1,0:T(8,128)} async-done(((f32[3072,256]{1,0:T(8,128)}), f32[96,256]{1,0:T(8,128)}) %reduce-scatter.7.cloned.1.call-update) | async-done | bytes 98320 | tf_op jit(solution)/shard_map/reduce_scatter | solution.py:68
  306.3 0.9 multiply_convert_fusion
  307.2 55.4 %all_gather.10 = bf16[1536,256]{1,0:T(8,128)(2,1)S(1)} all-gather(bf16[48,256]{1,0:T(8,128)(2,1)S(1)} %get-tuple-element.6), channel_id=1, replica_groups=mesh['fsdp'=32,'expert'=32] {'fsdp'}, dimensions={0}, use_global_device_ids=true | all-gather | bytes 811008 | tf_op jit(solution)/shard_map/all_gather | solution.py:97
  362.6 0.3 fusion.10
  363.0 49.7 %all_gather.11 = bf16[1536,256]{1,0:T(8,128)(2,1)S(1)} all-gather(bf16[48,256]{1,0:T(8,128)(2,1)S(1)} %get-tuple-element.5), channel_id=1, replica_groups=mesh['fsdp'=32,'expert'=32] {'fsdp'}, dimensions={0}, use_global_device_ids=true | all-gather | bytes 811008 | tf_op jit(solution)/shard_map/all_gather | solution.py:98
  412.7 0.3 convolution_add_fusion
  413.0 0.8 copy.96
  413.8 8.9 %all-to-all-start.3 = ((f32[32,8,192]{2,1,0:T(8,128)}), f32[32,8,192]{2,1,0:T(8,128)S(1)}, u32[]{:S(2)}, u32[]{:S(2)}) async-start(f32[32,8,192]{2,1,0:T(8,128)} %bitcast.20), calls=%async_computation.3 | async-start | bytes 524288 | tf_op jit(solution)/shard_map/all_to_all | solution.py:15
  422.7 53.9 %all_gather.9 = bf16[1536,256]{1,0:T(8,128)(2,1)S(1)} all-gather(bf16[48,256]{1,0:T(8,128)(2,1)S(1)} %get-tuple-element.7), channel_id=1, replica_groups=mesh['fsdp'=32,'expert'=32] {'fsdp'}, dimensions={0}, use_global_device_ids=true | all-gather | bytes 811008 | tf_op jit(solution)/shard_map/all_gather | solution.py:78
  476.7 1.2 copy.89
  477.8 2.4 fusion.4
  480.2 10.9 %all-to-all-start.1 = ((f32[32,8,192]{2,1,0:T(8,128)}), f32[32,8,192]{2,1,0:T(8,128)}, u32[]{:S(2)}, u32[]{:S(2)}) async-start(f32[32,8,192]{2,1,0:T(8,128)} %fusion.4), calls=%async_computation.1 | async-start | bytes 524288 | tf_op jit(solution)/shard_map/all_to_all | solution.py:15
  491.2 0.1 copy.81
  491.3 1.2 fusion
  492.5 1.2 fusion.1
  493.8 1.2 fusion.2
  495.0 0.8 convolution_reduce_fusion
  495.8 7.8 %all-to-all-done.1 = f32[32,8,192]{2,1,0:T(8,128)} async-done(((f32[32,8,192]{2,1,0:T(8,128)}), f32[32,8,192]{2,1,0:T(8,128)}, u32[]{:S(2)}, u32[]{:S(2)}) %all-to-all-start.1) | async-done | bytes 196640 | tf_op jit(solution)/shard_map/all_to_all | solution.py:15
  503.7 1.8 fusion.3
  (16 shorter events, 0.2 us)
Async XLA Ops:
  7.2 47.2 %copy-start = (bf16[1,192,1536]{2,1,0:T(8,128)(2,1)S(1)}, bf16[1,192,1536]{2,1,0:T(8,128)(2,1)}, u32[]{:S(2)}) copy-start(bf16[1,192,1536]{2,1,0:T(8,128)(2,1)} %param.15) | copy-start | bytes 1769476
  7.2 159.1 %reduce-scatter.9.cloned.1.call-start = ((), (), s32[]{:S(2)}) async-start(), calls=%async_computation.7 | async-start | bytes 1622016 | tf_op jit(solution)/shard_map/reduce_scatter | solution.py:87
  39.8 0.7 copy-start.3
  39.8 266.5 %reduce-scatter.7.cloned.1.call-start = ((), (), s32[]{:S(2)}) async-start(), calls=%async_computation.6 | async-start | bytes 3244032 | tf_op jit(solution)/shard_map/reduce_scatter | solution.py:68
  54.8 1.6 copy-start.1
  413.8 66.4 %all-to-all-start.3 = ((f32[32,8,192]{2,1,0:T(8,128)}), f32[32,8,192]{2,1,0:T(8,128)S(1)}, u32[]{:S(2)}, u32[]{:S(2)}) async-start(f32[32,8,192]{2,1,0:T(8,128)} %bitcast.20), calls=%async_computation.3 | async-start | bytes 524288 | tf_op jit(solution)/shard_map/all_to_all | solution.py:15
  480.2 23.4 %all-to-all-start.1 = ((f32[32,8,192]{2,1,0:T(8,128)}), f32[32,8,192]{2,1,0:T(8,128)}, u32[]{:S(2)}, u32[]{:S(2)}) async-start(f32[32,8,192]{2,1,0:T(8,128)} %fusion.4), calls=%async_computation.1 | async-start | bytes 524288 | tf_op jit(solution)/shard_map/all_to_all | solution.py:15
  492.5 11.1 %copy-start.2 = (f32[8,2]{0,1:T(2,128)S(1)}, f32[8,2]{0,1:T(2,128)}, u32[]{:S(2)}) copy-start(f32[8,2]{0,1:T(2,128)} %param.12) | copy-start | bytes 196
Sparse Core Ops, SparseCore 0:
  39.9 126.2 reduce-scatter.8
  171.9 134.3 reduce-scatter.6
where the time goes:
time: 513 us; the launch traced here: 512 us
  waiting for transfers between devices  252 us (49%)
  blocking collectives  198 us (39%)
  starting transfers between devices  19.9 us (4%)
  between operations  14.2 us (3%)
  matrix products  12 us (2%)
  local copies, waits for them, and re-layouts  10.7 us (2%)
  other arithmetic  5.79 us (1%)
    reduce_scatter x1, waiting for transfers between devices, per_device(): lax.psum_scatter(joined.reshape(lax.axis_size('fsdp') * (2 * share), slot...  140 us
    reduce_scatter x1, waiting for transfers between devices, per_device(): lax.psum_scatter(jnp.einsum('cd,rd->cr', down_rows, de_rows, preferred_el...  104 us
    all_gather x1, blocking collectives, per_device(): gate_piece = lax.all_gather(gate_grad, 'fsdp', axis=0, tiled=True)  55.4 us
    all_gather x1, blocking collectives, per_device(): piece = lax.all_gather(hidden, 'fsdp', axis=0, tiled=True)  53.9 us
    all_gather x1, blocking collectives, per_device(): up_piece = lax.all_gather(up_grad, 'fsdp', axis=0, tiled=True)  49.7 us
    all_to_all x2, blocking collectives, send_rows(): lax.all_to_all(buffer, 'expert', split_axis=0, concat_axis=0, tiled=True)  39.1 us
    all_to_all x2, starting transfers between devices, return_rows(): lax.all_to_all(buffer, 'expert', split_axis=0, concat_axis=0, tiled=True)  19.8 us
  transfers between devices with their start and end apart: 4, of which 3 were waited for; matrix products, arithmetic and copies ran while one was open for 3% of the time, Pallas kernels for 0%

commit v1 on v0

v1 whole, which is shorter than its diff:
```python
import jax
import jax.numpy as jnp
from jax import lax
from jax.experimental import pallas as pl
from jax.sharding import Mesh, PartitionSpec as P

EXPERTS = 4
DOMAINS = 8
CHUNKS = 1
INTERPRET = False
F32 = jnp.float32
LOW = jnp.bfloat16
NN = (((1,), (0,)), ((), ()))
NT = (((1,), (1,)), ((), ()))
TN = (((0,), (0,)), ((), ()))


def mm(a, b, dims):
    return lax.dot_general(a, b, dims, preferred_element_type=F32)


def partial_kernel(x_ref, g_ref, wg_ref, wu_ref, wd_ref, out_ref):
    width = wg_ref.shape[2]
    x = x_ref[...]
    out_ref[:, :width] = mm(x, wg_ref[0], NN).astype(LOW)
    out_ref[:, width : 2 * width] = mm(x, wu_ref[0], NN).astype(LOW)
    out_ref[:, 2 * width :] = mm(g_ref[...], wd_ref[0], NN).astype(LOW)


def middle_kernel(parts_ref, out_ref):
    copies, _, columns = parts_ref.shape
    width = columns // 3
    total = parts_ref[0].astype(F32)
    for i in range(1, copies):
        total = total + parts_ref[i].astype(F32)
    gate = total[:, :width]
    up = total[:, width : 2 * width]
    hidden_grad = total[:, 2 * width :]
    sigma = jax.nn.sigmoid(gate)
    hidden = (gate * sigma * up).astype(LOW)
    gate_grad = (hidden_grad * up * sigma * (1.0 + gate * (1.0 - sigma))).astype(LOW)
    up_grad = (hidden_grad * gate * sigma).astype(LOW)
    for i in range(copies):
        out_ref[i, :, :width] = hidden
        out_ref[i, :, width : 2 * width] = gate_grad
        out_ref[i, :, 2 * width :] = up_grad


def rows_kernel(*refs):
    acts, (wg_ref, wu_ref, wd_ref, out_ref, in_ref) = refs[:-5], refs[-5:]
    out = None
    for i, act_ref in enumerate(acts):
        width = act_ref.shape[1] // 3
        cols = slice(i * width, (i + 1) * width)
        o = mm(act_ref[:, :width], wd_ref[0, :, cols], NT)
        g = mm(act_ref[:, width : 2 * width], wg_ref[0, :, cols], NT)
        g = g + mm(act_ref[:, 2 * width :], wu_ref[0, :, cols], NT)
        out, back = (o, g) if out is None else (out + o, back + g)
    out_ref[...] = out.astype(LOW)
    in_ref[...] = back.astype(LOW)


def grads_kernel(*refs):
    acts, (x_ref, g_ref, gg_ref, gu_ref, gd_ref) = refs[:-5], refs[-5:]
    for i, act_ref in enumerate(acts):
        width = act_ref.shape[1] // 3
        cols = slice(i * width, (i + 1) * width)
        gd_ref[0, :, cols] = mm(g_ref[...], act_ref[:, :width], TN).astype(LOW)
        gg_ref[0, :, cols] = mm(x_ref[...], act_ref[:, width : 2 * width], TN).astype(LOW)
        gu_ref[0, :, cols] = mm(x_ref[...], act_ref[:, 2 * width :], TN).astype(LOW)


def call(kernel, shapes, *args, **extra):
    return pl.pallas_call(kernel, out_shape=shapes, interpret=INTERPRET, **extra)(*args)


def exchange(value, axis):
    return lax.all_to_all(value, axis, split_axis=0, concat_axis=0, tiled=True)


def scatter_sum(value, axis, count):
    rows, columns = value.shape
    parts = exchange(value.reshape(count, rows // count, columns), axis)
    return jnp.sum(parts.astype(F32), axis=0).astype(LOW)


def gather_rows(value, axis, count):
    rows, columns = value.shape
    copies = jnp.broadcast_to(value[None], (count, rows, columns))
    return exchange(copies, axis).reshape(count * rows, columns)


def per_device(
    tokens, cotangent, routes, route_weights, domains, loss_weights, w_gate, w_up, w_down
):
    tok_count, local_width = tokens.shape
    n_x, n_z, n_core = lax.axis_size("x"), lax.axis_size("z_hi"), lax.axis_size("core")
    groups = lax.axis_size("y")
    owners = EXPERTS * groups
    rows = owners * tok_count
    grp_width = w_gate.shape[2]
    width = grp_width // CHUNKS
    w_down_t = jnp.swapaxes(w_down, 1, 2)

    named = routes[None, :, :] == jnp.arange(EXPERTS, dtype=jnp.int32)[:, None, None]
    chosen = jnp.any(named, axis=2)
    weight = jnp.sum(jnp.where(named, route_weights[None], F32(0.0)), axis=2)
    domain_hit = domains[:, None] == jnp.arange(DOMAINS, dtype=jnp.int32)[None, :]
    token_scale = jnp.sum(jnp.where(domain_hit, loss_weights[None, :], F32(0.0)), axis=1)
    scaled = (cotangent.astype(F32) * token_scale[:, None]).astype(LOW)
    send_x = jnp.where(chosen[:, :, None], tokens[None], jnp.zeros((), LOW))
    send_g = (weight[:, :, None] * scaled[None].astype(F32)).astype(LOW)
    send = jnp.stack([send_x, send_g], axis=1)
    send = jnp.broadcast_to(send[:, None], (EXPERTS, groups, 2, tok_count, local_width))
    got = exchange(send.reshape(owners, 2, tok_count, local_width), ("z_lo", "y"))
    x_rows = got[:, 0].reshape(rows, local_width)
    g_rows = got[:, 1].reshape(rows, local_width)

    acts = []
    for chunk in range(CHUNKS):
        whole = pl.BlockSpec((rows, local_width), lambda i: (0, 0))
        part = pl.BlockSpec((1, local_width, width), lambda i, chunk=chunk: (0, 0, chunk))
        sums = call(
            partial_kernel,
            jax.ShapeDtypeStruct((rows, 3 * width), LOW),
            x_rows,
            g_rows,
            w_gate,
            w_up,
            w_down_t,
            grid=(1,),
            in_specs=[whole, whole, part, part, part],
            out_specs=pl.BlockSpec((rows, 3 * width), lambda i: (0, 0)),
        )
        sums = scatter_sum(sums, "core", n_core)
        sums = scatter_sum(sums, "x", n_x)
        last = sums.shape[0] // n_z
        parts = exchange(sums.reshape(n_z, last, 3 * width), "z_hi")
        copies = call(middle_kernel, jax.ShapeDtypeStruct(parts.shape, LOW), parts)
        act = exchange(copies, "z_hi").reshape(n_z * last, 3 * width)
        act = gather_rows(act, "x", n_x)
        act = gather_rows(act, "core", n_core)
        acts.append(act)

    flat = jax.ShapeDtypeStruct((rows, local_width), LOW)
    out_part, in_part = call(rows_kernel, (flat, flat), *acts, w_gate, w_up, w_down_t)
    back = jnp.stack(
        [
            out_part.reshape(owners, tok_count, local_width),
            in_part.reshape(owners, tok_count, local_width),
        ],
        axis=1,
    )
    back = exchange(back, ("z_lo", "y"))
    grad = jax.ShapeDtypeStruct((1, local_width, grp_width), LOW)
    grad_gate, grad_up, grad_down = call(grads_kernel, (grad, grad, grad), *acts, x_rows, g_rows)
    back = back.reshape(EXPERTS, groups, 2, tok_count, local_width).astype(F32)
    mixed = jnp.sum(weight[:, :, None] * jnp.sum(back[:, :, 0], axis=1), axis=0)
    grad_tokens = jnp.sum(back[:, :, 1], axis=(0, 1))
    return (
        mixed.astype(LOW),
        grad_tokens.astype(LOW),
        grad_gate,
        grad_up,
        jnp.swapaxes(grad_down, 1, 2),
    )


def solution(mesh):
    n_fsdp, n_expert = mesh.shape["fsdp"], mesh.shape["expert"]
    n_x = 4 if n_fsdp >= 32 else 2
    split = (n_x, n_fsdp // (2 * n_x), 2, EXPERTS, n_expert // EXPERTS)
    fine = Mesh(mesh.devices.reshape(split), ("x", "z_hi", "core", "z_lo", "y"))
    fsdp, expert = ("x", "z_hi", "core"), ("z_lo", "y")
    in_specs = (
        P(expert, fsdp),
        P(expert, fsdp),
        P(expert, None),
        P(expert, None),
        P(expert),
        P(),
        P(expert, fsdp, None),
        P(expert, fsdp, None),
        P(expert, None, fsdp),
    )
    out_specs = (
        P(expert, fsdp),
        P(expert, fsdp),
        P(expert, fsdp, None),
        P(expert, fsdp, None),
        P(expert, None, fsdp),
    )
    return jax.shard_map(
        per_device, mesh=fine, in_specs=in_specs, out_specs=out_specs, check_vma=False
    )
```

time: 513 us -> 175 us (0.34)
  waiting for transfers between devices: 252 us -> 8.79 us
  blocking collectives: 198 us -> 135 us
  between operations: 14.2 us -> 0.68 us
  Pallas kernels: 0 us -> 12.5 us
  matrix products: 12 us -> 0 us
  starting transfers between devices: 19.9 us -> 8.91 us
  local copies, waits for them, and re-layouts: 10.7 us -> 0.97 us
    reduce_scatter x2 -> x0, waiting for transfers between devices: 244 us -> none  [the longest x1 140 us: per_device(): lax.psum_scatter(joined.reshape(lax.axis_size('fsdp') * (2 * share), slot...]
    all_gather x3 -> x0, blocking collectives: 159 us -> none  [the longest x1 55.4 us: per_device(): gate_piece = lax.all_gather(gate_grad, 'fsdp', axis=0, tiled=True)]
    all_to_all x2 -> x7, blocking collectives: 39.1 us -> 135 us  [exchange(): return lax.all_to_all(value, axis, split_axis=0, concat_axis=0, tiled=True)]
    pallas_call x0 -> x4, Pallas kernels: none -> 12.5 us  [call(): pl.pallas_call(kernel, out_shape=shapes, interpret=INTERPRET, **extra)]
    dot_general x13 -> x0, matrix products: 12 us -> none  [the longest x1 2.41 us: per_device(): jnp.einsum('nr,nd->rd', piece, down_rows, preferred_element_type=jnp.floa...]
    all_to_all x2 -> x1, starting transfers between devices: 19.8 us -> 8.91 us  [exchange(): return lax.all_to_all(value, axis, split_axis=0, concat_axis=0, tiled=True)]
  transfers between devices with their start and end apart: 4 -> 1, of which waited for: 3 -> 1; matrix products, arithmetic and copies ran while one was open for 3% -> 0% of each run, Pallas kernels for 0% -> 2%
where the time goes in v1:
time: 175 us
  blocking collectives  135 us (77%)
  Pallas kernels  12.5 us (7%)
  starting transfers between devices  8.91 us (5%)
  waiting for transfers between devices  8.79 us (5%)
  other arithmetic  7.94 us (5%)
    all_to_all x7, blocking collectives, exchange(): return lax.all_to_all(value, axis, split_axis=0, concat_axis=0, tiled=True)  135 us
    pallas_call x4, Pallas kernels, call(): pl.pallas_call(kernel, out_shape=shapes, interpret=INTERPRET, **extra)  12.5 us
    all_to_all x1, starting transfers between devices, exchange(): return lax.all_to_all(value, axis, split_axis=0, concat_axis=0, tiled=True)  8.91 us
    all_to_all x1, waiting for transfers between devices, exchange(): return lax.all_to_all(value, axis, split_axis=0, concat_axis=0, tiled=True)  8.79 us
  transfers between devices with their start and end apart: 1, of which 1 were waited for; matrix products, arithmetic and copies ran while one was open for 0% of the time, Pallas kernels for 2%

profile of v1, /device:TPU:8, one launch (start us, length us, event | category | flops | bytes accessed | tf_op | source)
XLA Modules:
  0.0 174.6 jit_solution(6033740429528949731)
XLA Ops:
  0.6 0.7 fusion.1
  1.3 0.7 select_reduce_fusion.1
  2.0 0.9 select_reduce_fusion
  2.9 0.8 fusion
  3.6 0.1 multiply_convert_fusion
  3.7 0.8 broadcast_select_fusion
  4.5 26.3 %all_to_all.40 = bf16[32,2,8,192]{3,2,1,0:T(8,128)(2,1)S(1)} all-to-all(bf16[32,2,8,192]{3,2,1,0:T(8,128)(2,1)S(1)} %bitcast.31), channel_id=1, replica_groups=mesh['x'=4,'z_hi'=4,'core'=2,'z_lo'=4,'y'=8] {'z_lo','y'}, dimensions={0} | all-to-all | bytes 393216 | tf_op jit(solution)/shard_map/all_to_all | solution.py:78
  30.9 0.7 slice_bitcast_fusion
  31.6 3.7 %shard_map.128 = bf16[256,4608]{1,0:T(8,128)(2,1)} custom-call(bf16[256,192]{1,0:T(8,128)(2,1)} %get-tuple-element.18.x_ref.refs_1_, bf16[256,192]{1,0:T(8,128)(2,1)} %get-tuple-element.17.g_ref.refs_2_, bf16[1,192,1536]{2,1,0:T(8,128)(2,1)} %refs_1_.1, bf16[1,192,1536]{2,1,0:T(8,128)(2,1)} %refs_2_.1, bf16[1,192,1536]{2,1,0:T(8,128)(2,1)} %bitcast.27), custom_call_target="tpu_custom_call" | custom-call | tf_op jit(solution)/shard_map/pallas_call | solution.py:74
  35.3 6.8 %all_to_all.41 = bf16[2,128,4608]{2,1,0:T(8,128)(2,1)S(1)} all-to-all(bf16[2,128,4608]{2,1,0:T(8,128)(2,1)} %bitcast.24), channel_id=1, replica_groups=mesh['x'=4,'z_hi'=4,'core'=2,'z_lo'=4,'y'=8] {'core'}, dimensions={0} | all-to-all | bytes 4718592 | tf_op jit(solution)/shard_map/all_to_all | solution.py:78
  42.1 0.8 reduce_sum.71
  42.9 19.5 %all_to_all.42 = bf16[4,32,4608]{2,1,0:T(8,128)(2,1)S(1)} all-to-all(bf16[4,32,4608]{2,1,0:T(8,128)(2,1)S(1)} %bitcast.26), channel_id=1, replica_groups=mesh['x'=4,'z_hi'=4,'core'=2,'z_lo'=4,'y'=8] {'x'}, dimensions={0} | all-to-all | bytes 2359296 | tf_op jit(solution)/shard_map/all_to_all | solution.py:78
  62.4 0.3 reduce_sum.72
  62.7 36.0 %all_to_all.43.parts_ref = bf16[4,8,4608]{2,1,0:T(8,128)(2,1)} all-to-all(bf16[4,8,4608]{2,1,0:T(8,128)(2,1)S(1)} %bitcast.29), channel_id=1, replica_groups=mesh['x'=4,'z_hi'=4,'core'=2,'z_lo'=4,'y'=8] {'z_hi'}, dimensions={0} | all-to-all | bytes 589824 | tf_op jit(solution)/shard_map/all_to_all | solution.py:78
  98.6 1.7 shard_map.129
  100.4 24.6 %all_to_all.44 = bf16[4,8,4608]{2,1,0:T(8,128)(2,1)S(1)} all-to-all(bf16[4,8,4608]{2,1,0:T(8,128)(2,1)} %shard_map.129), channel_id=1, replica_groups=mesh['x'=4,'z_hi'=4,'core'=2,'z_lo'=4,'y'=8] {'z_hi'}, dimensions={0} | all-to-all | bytes 589824 | tf_op jit(solution)/shard_map/all_to_all | solution.py:78
  125.0 0.1 broadcast_in_dim.85
  125.1 15.0 %all_to_all.45 = bf16[4,32,4608]{2,1,0:T(8,128)(2,1)S(1)} all-to-all(bf16[4,32,4608]{2,1,0:T(8,128)(2,1)S(1)} %broadcast_in_dim.85), channel_id=1, replica_groups=mesh['x'=4,'z_hi'=4,'core'=2,'z_lo'=4,'y'=8] {'x'}, dimensions={0} | all-to-all | bytes 2359296 | tf_op jit(solution)/shard_map/all_to_all | solution.py:78
  140.1 0.2 broadcast_in_dim.87
  140.3 6.5 %all_to_all.46 = bf16[2,128,4608]{2,1,0:T(8,128)(2,1)} all-to-all(bf16[2,128,4608]{2,1,0:T(8,128)(2,1)S(1)} %broadcast_in_dim.87), channel_id=1, replica_groups=mesh['x'=4,'z_hi'=4,'core'=2,'z_lo'=4,'y'=8] {'core'}, dimensions={0} | all-to-all | bytes 4718592 | tf_op jit(solution)/shard_map/all_to_all | solution.py:78
  146.8 3.6 %shard_map.130 = (bf16[256,192]{1,0:T(8,128)(2,1)}, bf16[256,192]{1,0:T(8,128)(2,1)}) custom-call(bf16[256,4608]{1,0:T(8,128)(2,1)} %bitcast.22, bf16[1,192,1536]{2,1,0:T(8,128)(2,1)} %refs_1_.1, bf16[1,192,1536]{2,1,0:T(8,128)(2,1)} %refs_2_.1, bf16[1,192,1536]{2,1,0:T(8,128)(2,1)} %bitcast.28), custom_call_target="tpu_custom_call" | custom-call | tf_op jit(solution)/shard_map/pallas_call | solution.py:74
  150.4 1.7 pad_maximum_fusion
  152.1 8.9 %all-to-all-start.7 = ((bf16[32,2,8,192]{3,2,1,0:T(8,128)(2,1)}), bf16[32,2,8,192]{3,2,1,0:T(8,128)(2,1)S(1)}, u32[]{:S(2)}, u32[]{:S(2)}) async-start(bf16[32,2,8,192]{3,2,1,0:T(8,128)(2,1)} %pad_maximum_fusion), calls=%async_computation.7 | async-start | bytes 524288 | tf_op jit(solution)/shard_map/all_to_all | solution.py:78
  161.0 3.5 %shard_map.131 = (bf16[1,192,1536]{2,1,0:T(8,128)(2,1)}, bf16[1,192,1536]{2,1,0:T(8,128)(2,1)}, bf16[1,192,1536]{2,1,0:T(8,128)(2,1)}) custom-call(bf16[256,4608]{1,0:T(8,128)(2,1)} %bitcast.23, bf16[256,192]{1,0:T(8,128)(2,1)} %get-tuple-element.18.x_ref.refs_1_, bf16[256,192]{1,0:T(8,128)(2,1)} %get-tuple-element.17.g_ref.refs_2_), custom_call_target="tpu_custom_call" | custom-call | tf_op jit(solution)/shard_map/pallas_call | solution.py:74
  164.5 8.8 %all-to-all-done.7 = bf16[32,2,8,192]{3,2,1,0:T(8,128)(2,1)S(1)} async-done(((bf16[32,2,8,192]{3,2,1,0:T(8,128)(2,1)}), bf16[32,2,8,192]{3,2,1,0:T(8,128)(2,1)S(1)}, u32[]{:S(2)}, u32[]{:S(2)}) %all-to-all-start.7) | async-done | bytes 196640 | tf_op jit(solution)/shard_map/all_to_all | solution.py:78
  173.3 0.6 slice_reduce_fusion
  174.0 0.7 multiply_reduce_fusion
  (3 shorter events, 0.1 us)
Async XLA Ops:
  152.1 21.2 %all-to-all-start.7 = ((bf16[32,2,8,192]{3,2,1,0:T(8,128)(2,1)}), bf16[32,2,8,192]{3,2,1,0:T(8,128)(2,1)S(1)}, u32[]{:S(2)}, u32[]{:S(2)}) async-start(bf16[32,2,8,192]{3,2,1,0:T(8,128)(2,1)} %pad_maximum_fusion), calls=%async_computation.7 | async-start | bytes 524288 | tf_op jit(solution)/shard_map/all_to_all | solution.py:78

commit v2 on v1

v2 whole, which is shorter than its diff:
```python
import jax
import jax.numpy as jnp
from jax import lax
from jax.experimental import pallas as pl
from jax.experimental.pallas import tpu as pltpu
from jax.sharding import Mesh, PartitionSpec as P

EXPERTS = 4
TOP = 2
BLOCK_COLS = 512
INTERPRET = False
F32 = jnp.float32
LOW = jnp.bfloat16
NN = (((1,), (0,)), ((), ()))
NT = (((1,), (1,)), ((), ()))
TN = (((0,), (0,)), ((), ()))


def mm(a, b, dims):
    return lax.dot_general(a, b, dims, preferred_element_type=F32)


def column(values):
    spots = lax.broadcasted_iota(jnp.int32, (len(values), 1), 0)
    out = jnp.zeros((len(values), 1), F32)
    for t, value in enumerate(values):
        out = jnp.where(spots == t, value, out)
    return out


def expert_column(routes_ref, values, expert, count):
    picked = []
    for t in range(count):
        total = F32(0.0)
        for k in range(TOP):
            total = total + jnp.where(routes_ref[k, t] == expert, values(k, t), F32(0.0))
        picked.append(total)
    return column(picked)


def send_kernel(routes_ref, weights_ref, domains_ref, loss_ref, tok_ref, cot_ref, out_ref):
    count = tok_ref.shape[0]
    groups = out_ref.shape[0] // EXPERTS
    scale = column([loss_ref[domains_ref[t]] for t in range(count)])
    scaled = (cot_ref[...].astype(F32) * scale).astype(LOW).astype(F32)
    tok = tok_ref[...].astype(F32)
    for expert in range(EXPERTS):
        weight = expert_column(routes_ref, lambda k, t: weights_ref[k, t], expert, count)
        named = expert_column(routes_ref, lambda k, t: F32(1.0), expert, count)
        x_part = jnp.where(named > 0.0, tok, F32(0.0)).astype(LOW)
        g_part = (weight * scaled).astype(LOW)
        for group in range(groups):
            out_ref[expert * groups + group, 0] = x_part
            out_ref[expert * groups + group, 1] = g_part


def final_kernel(routes_ref, weights_ref, back_ref, mixed_ref, grad_ref):
    count = back_ref.shape[2]
    groups = back_ref.shape[0] // EXPERTS
    mixed, grad = None, None
    for expert in range(EXPERTS):
        weight = expert_column(routes_ref, lambda k, t: weights_ref[k, t], expert, count)
        out = back_ref[expert * groups, 0].astype(F32)
        inner = back_ref[expert * groups, 1].astype(F32)
        for group in range(1, groups):
            out = out + back_ref[expert * groups + group, 0].astype(F32)
            inner = inner + back_ref[expert * groups + group, 1].astype(F32)
        out = weight * out
        mixed = out if mixed is None else mixed + out
        grad = inner if grad is None else grad + inner
    mixed_ref[...] = mixed.astype(LOW)
    grad_ref[...] = grad.astype(LOW)


def rows_of(ref, which):
    blocks, _, count, width = ref.shape
    return ref[:, which].reshape(blocks * count, width)


def partial_kernel(half_ref, got_ref, wg_ref, wu_ref, wd_ref, out_ref):
    width = wg_ref.shape[2]
    x = rows_of(got_ref, 0)
    out_ref[:, :width] = mm(x, wg_ref[0], NN).astype(LOW)
    out_ref[:, width : 2 * width] = mm(x, wu_ref[0], NN).astype(LOW)
    out_ref[:, 2 * width :] = mm(rows_of(got_ref, 1), wd_ref[0], NN).astype(LOW)


def middle_kernel(parts_ref, out_ref):
    copies, _, columns = parts_ref.shape
    for start in range(0, columns, 3 * BLOCK_COLS):
        cols = [
            slice(start + i * BLOCK_COLS, start + (i + 1) * BLOCK_COLS) for i in range(3)
        ]
        sums = []
        for col in cols:
            total = parts_ref[0, :, col].astype(F32)
            for i in range(1, copies):
                total = total + parts_ref[i, :, col].astype(F32)
            sums.append(total)
        gate, up, hidden_grad = sums
        sigma = jax.nn.sigmoid(gate)
        hidden = (gate * sigma * up).astype(LOW)
        gate_grad = (hidden_grad * up * sigma * (1.0 + gate * (1.0 - sigma))).astype(LOW)
        up_grad = (hidden_grad * gate * sigma).astype(LOW)
        for i in range(copies):
            for col, value in zip(cols, (hidden, gate_grad, up_grad)):
                out_ref[i, :, col] = value


def row_products(act_ref, wg_ref, wu_ref, wd_ref, out_acc, in_acc):
    width = wg_ref.shape[2]
    step = pl.program_id(0)

    @pl.when(step == 0)
    def _():
        out_acc[...] = jnp.zeros_like(out_acc)
        in_acc[...] = jnp.zeros_like(in_acc)

    out_acc[...] += mm(act_ref[:, :width], wd_ref[0], NT)
    inner = mm(act_ref[:, width : 2 * width], wg_ref[0], NT)
    in_acc[...] += inner + mm(act_ref[:, 2 * width :], wu_ref[0], NT)


def store_rows(back_ref, out_acc, in_acc):
    blocks, _, count, width = back_ref.shape

    @pl.when(pl.program_id(0) == pl.num_programs(0) - 1)
    def _():
        back_ref[:, 0] = out_acc[...].reshape(blocks, count, width).astype(LOW)
        back_ref[:, 1] = in_acc[...].reshape(blocks, count, width).astype(LOW)


def own_kernel(half_ref, act_ref, wg_ref, wu_ref, wd_ref, back_ref, out_acc, in_acc):
    row_products(act_ref, wg_ref, wu_ref, wd_ref, out_acc, in_acc)
    store_rows(back_ref, out_acc, in_acc)


def tail_kernel(
    half_ref,
    own_ref,
    other_ref,
    own_got_ref,
    other_got_ref,
    wg_ref,
    wu_ref,
    wd_ref,
    held_ref,
    back_ref,
    gg_ref,
    gu_ref,
    gd_ref,
    out_acc,
    in_acc,
):
    width = wg_ref.shape[2]
    row_products(other_ref, wg_ref, wu_ref, wd_ref, out_acc, in_acc)
    x = jnp.concatenate([rows_of(own_got_ref, 0), rows_of(other_got_ref, 0)], axis=0)
    g = jnp.concatenate([rows_of(own_got_ref, 1), rows_of(other_got_ref, 1)], axis=0)
    act = jnp.concatenate([own_ref[...], other_ref[...]], axis=0)
    gd_ref[0] = mm(g, act[:, :width], TN).astype(LOW)
    gg_ref[0] = mm(x, act[:, width : 2 * width], TN).astype(LOW)
    gu_ref[0] = mm(x, act[:, 2 * width :], TN).astype(LOW)
    store_rows(back_ref, out_acc, in_acc)


def exchange(value, axis):
    return lax.all_to_all(value, axis, split_axis=0, concat_axis=0, tiled=True)


def per_device(
    tokens, cotangent, routes, route_weights, domains, loss_weights, w_gate, w_up, w_down
):
    tok_count, local_width = tokens.shape
    n_x, n_z, n_core = lax.axis_size("x"), lax.axis_size("z_hi"), lax.axis_size("core")
    owners = EXPERTS * lax.axis_size("y")
    grp_width = w_gate.shape[2]
    steps = grp_width // BLOCK_COLS
    columns = 3 * grp_width
    half_rows = owners * tok_count // n_core
    w_down_t = jnp.swapaxes(w_down, 1, 2)
    routes_t = routes.T
    weights_t = route_weights.T
    half = lax.axis_index("core").reshape(1).astype(jnp.int32)
    swap = [(0, 1), (1, 0)]

    small = pl.BlockSpec(memory_space=pltpu.SMEM)
    plain = pl.BlockSpec(memory_space=pltpu.VMEM)
    flat = jax.ShapeDtypeStruct((tok_count, local_width), LOW)
    block = jax.ShapeDtypeStruct((owners, 2, tok_count, local_width), LOW)
    send = pl.pallas_call(
        send_kernel,
        out_shape=block,
        in_specs=[small, small, small, small, plain, plain],
        interpret=INTERPRET,
    )(routes_t, weights_t, domains, loss_weights, tokens, cotangent)
    send, half = lax.optimization_barrier((send, half))
    got = exchange(send, ("z_lo", "y"))

    def quarter(other):
        return pl.BlockSpec(
            (owners // n_core, 2, tok_count, local_width),
            lambda j, half_ref: (1 - half_ref[0] if other else half_ref[0], 0, 0, 0),
        )

    weight = pl.BlockSpec((1, local_width, BLOCK_COLS), lambda j, half_ref: (0, 0, j))
    act_spec = pl.BlockSpec((half_rows, 3 * BLOCK_COLS), lambda j, half_ref: (0, j))
    anywhere = pl.BlockSpec(memory_space=pl.ANY)
    accs = [pltpu.VMEM((half_rows, local_width), F32)] * 2

    def run(kernel, in_specs, out_specs, shapes, scratch, aliases, *args):
        return pl.pallas_call(
            kernel,
            out_shape=shapes,
            grid_spec=pltpu.PrefetchScalarGridSpec(
                num_scalar_prefetch=1,
                grid=(steps,),
                in_specs=in_specs,
                out_specs=out_specs,
                scratch_shapes=scratch,
            ),
            input_output_aliases=aliases,
            interpret=INTERPRET,
        )(half, *args)

    def partial(other):
        return run(
            partial_kernel,
            [quarter(other), weight, weight, weight],
            act_spec,
            jax.ShapeDtypeStruct((half_rows, columns), LOW),
            [],
            {},
            got,
            w_gate,
            w_up,
            w_down_t,
        )

    arrived = lax.ppermute(partial(True), "core", swap)
    sums = (partial(False).astype(F32) + arrived.astype(F32)).astype(LOW)
    parts = exchange(sums.reshape(n_x, half_rows // n_x, columns), "x")
    sums = jnp.sum(parts.astype(F32), axis=0).astype(LOW)
    parts = exchange(sums.reshape(n_z, sums.shape[0] // n_z, columns), "z_hi")
    copies = pl.pallas_call(
        middle_kernel, out_shape=jax.ShapeDtypeStruct(parts.shape, LOW), interpret=INTERPRET
    )(parts)
    act = exchange(copies, "z_hi").reshape(1, half_rows // n_x, columns)
    act = exchange(jnp.broadcast_to(act, (n_x,) + act.shape[1:]), "x")
    own = act.reshape(half_rows, columns)
    other = lax.ppermute(own, "core", swap)

    back = run(
        own_kernel,
        [act_spec, weight, weight, weight],
        quarter(False),
        block,
        accs,
        {},
        own,
        w_gate,
        w_up,
        w_down_t,
    )
    grad = jax.ShapeDtypeStruct((1, local_width, grp_width), LOW)
    back, grad_gate, grad_up, grad_down = run(
        tail_kernel,
        [act_spec, act_spec, quarter(False), quarter(True), weight, weight, weight, anywhere],
        [quarter(True), weight, weight, weight],
        (block, grad, grad, grad),
        accs,
        {8: 0},
        own,
        other,
        got,
        got,
        w_gate,
        w_up,
        w_down_t,
        back,
    )
    back = exchange(back, ("z_lo", "y"))
    mixed, grad_tokens = pl.pallas_call(
        final_kernel,
        out_shape=(flat, flat),
        in_specs=[small, small, plain],
        interpret=INTERPRET,
    )(routes_t, weights_t, back)
    return mixed, grad_tokens, grad_gate, grad_up, jnp.swapaxes(grad_down, 1, 2)


def solution(mesh):
    n_fsdp, n_expert = mesh.shape["fsdp"], mesh.shape["expert"]
    n_x = 4 if n_fsdp >= 32 else 2
    split = (n_x, n_fsdp // (2 * n_x), 2, EXPERTS, n_expert // EXPERTS)
    fine = Mesh(mesh.devices.reshape(split), ("x", "z_hi", "core", "z_lo", "y"))
    fsdp, expert = ("x", "z_hi", "core"), ("z_lo", "y")
    in_specs = (
        P(expert, fsdp),
        P(expert, fsdp),
        P(expert, None),
        P(expert, None),
        P(expert),
        P(),
        P(expert, fsdp, None),
        P(expert, fsdp, None),
        P(expert, None, fsdp),
    )
    out_specs = (
        P(expert, fsdp),
        P(expert, fsdp),
        P(expert, fsdp, None),
        P(expert, fsdp, None),
        P(expert, None, fsdp),
    )
    return jax.shard_map(
        per_device, mesh=fine, in_specs=in_specs, out_specs=out_specs, check_vma=False
    )
```

time: 175 us -> 175 us (level)
  blocking collectives: 135 us -> 145 us
  Pallas kernels: 12.5 us -> 22 us
  waiting for transfers between devices: 8.79 us -> 0.01 us
  other arithmetic: 7.94 us -> 1.79 us
  starting transfers between devices: 8.91 us -> 3.82 us
    all_to_all x7 -> x6, blocking collectives: 135 us -> 145 us  [exchange(): return lax.all_to_all(value, axis, split_axis=0, concat_axis=0, tiled=True)]
    pallas_call x4 -> x7, Pallas kernels: 12.5 us -> 22 us  [the longest x4 17.1 us: run(): pl.pallas_call(kernel, out_shape=shapes, grid_spec=pltpu.PrefetchScalarGr...]
    all_to_all x1 -> x0, starting transfers between devices: 8.91 us -> none  [exchange(): return lax.all_to_all(value, axis, split_axis=0, concat_axis=0, tiled=True)]
    all_to_all x1 -> x0, waiting for transfers between devices: 8.79 us -> none  [exchange(): return lax.all_to_all(value, axis, split_axis=0, concat_axis=0, tiled=True)]
    ppermute x0 -> x2, starting transfers between devices: none -> 3.82 us  [the longest x1 1.91 us: per_device(): other = lax.ppermute(own, 'core', swap)]
    reduce_sum x6 -> x1, other arithmetic: 3.88 us -> 0.25 us  [per_device(): sums = jnp.sum(parts.astype(F32), axis=0).astype(LOW)]
  transfers between devices with their start and end apart: 1 -> 2, of which waited for: 1 -> 0; matrix products, arithmetic and copies ran while one was open for 0% -> 0% of each run, Pallas kernels for 2% -> 4%
where the time goes in v2:
time: 175 us; the launch traced here: 174 us
  blocking collectives  145 us (83%)
  Pallas kernels  22 us (13%)
  starting transfers between devices  3.82 us (2%)
  other arithmetic  1.79 us (1%)
    all_to_all x6, blocking collectives, exchange(): return lax.all_to_all(value, axis, split_axis=0, concat_axis=0, tiled=True)  145 us
    pallas_call x4, Pallas kernels, run(): pl.pallas_call(kernel, out_shape=shapes, grid_spec=pltpu.PrefetchScalarGr...  17.1 us
  transfers between devices with their start and end apart: 2, of which 0 were waited for; matrix products, arithmetic and copies ran while one was open for 0% of the time, Pallas kernels for 4%

profile of v2, /device:TPU:8, one launch (start us, length us, event | category | flops | bytes accessed | tf_op | source)
XLA Modules:
  0.0 174.3 jit_solution(3444083588450045256)
XLA Ops:
  0.6 1.6 shard_map.128
  2.2 27.9 %all_to_all.30.got_ref.own_got_ref.other_got_ref = bf16[32,2,8,192]{3,2,1,0:T(8,128)(2,1)} all-to-all(bf16[32,2,8,192]{3,2,1,0:T(8,128)(2,1)} %shard_map.128), channel_id=1, replica_groups=mesh['x'=4,'z_hi'=4,'core'=2,'z_lo'=4,'y'=8] {'z_lo','y'}, dimensions={0} | all-to-all | bytes 393216 | tf_op jit(solution)/shard_map/all_to_all | solution.py:167
  30.1 4.0 %shard_map.130 = bf16[128,4608]{1,0:T(8,128)(2,1)} custom-call(s32[1]{0:T(128)} %bitcast.2.half_ref, bf16[32,2,8,192]{3,2,1,0:T(8,128)(2,1)} %all_to_all.30.got_ref.own_got_ref.other_got_ref, bf16[1,192,1536]{2,1,0:T(8,128)(2,1)} %wg_ref.7, bf16[1,192,1536]{2,1,0:T(8,128)(2,1)} %wu_ref.7, bf16[1,192,1536]{2,1,0:T(8,128)(2,1)} %bitcast.12), custom_call_target="tpu_custom_call" | custom-call | tf_op jit(solution)/shard_map/pallas_call | solution.py:211
  34.1 1.9 %collective-permute-start = (bf16[128,4608]{1,0:T(8,128)(2,1)}, bf16[128,4608]{1,0:T(8,128)(2,1)S(1)}, u32[]{:S(2)}, u32[]{:S(2)}) collective-permute-start(bf16[128,4608]{1,0:T(8,128)(2,1)} %shard_map.130), channel_id=1, source_target_pairs={{0,32},{32,0},{1,33},{33,1},{2,34},{34,2},{3,35},{35,3},{4,36},{36... | collective-permute-start | bytes 3538952 | tf_op jit(solution)/shard_map/ppermute | solution.py:239
  36.0 4.0 %shard_map.129 = bf16[128,4608]{1,0:T(8,128)(2,1)} custom-call(s32[1]{0:T(128)} %bitcast.2.half_ref, bf16[32,2,8,192]{3,2,1,0:T(8,128)(2,1)} %all_to_all.30.got_ref.own_got_ref.other_got_ref, bf16[1,192,1536]{2,1,0:T(8,128)(2,1)} %wg_ref.7, bf16[1,192,1536]{2,1,0:T(8,128)(2,1)} %wu_ref.7, bf16[1,192,1536]{2,1,0:T(8,128)(2,1)} %bitcast.13), custom_call_target="tpu_custom_call" | custom-call | tf_op jit(solution)/shard_map/pallas_call | solution.py:211
  40.0 0.0 collective-permute-done
  40.1 1.5 add_convert_fusion
  41.6 19.9 %all_to_all.31 = bf16[4,32,4608]{2,1,0:T(8,128)(2,1)S(1)} all-to-all(bf16[4,32,4608]{2,1,0:T(8,128)(2,1)S(1)} %bitcast.16), channel_id=1, replica_groups=mesh['x'=4,'z_hi'=4,'core'=2,'z_lo'=4,'y'=8] {'x'}, dimensions={0} | all-to-all | bytes 2359296 | tf_op jit(solution)/shard_map/all_to_all | solution.py:167
  61.5 0.3 reduce_sum.12
  61.7 35.0 %all_to_all.32.parts_ref = bf16[4,8,4608]{2,1,0:T(8,128)(2,1)} all-to-all(bf16[4,8,4608]{2,1,0:T(8,128)(2,1)S(1)} %bitcast.17), channel_id=1, replica_groups=mesh['x'=4,'z_hi'=4,'core'=2,'z_lo'=4,'y'=8] {'z_hi'}, dimensions={0} | all-to-all | bytes 589824 | tf_op jit(solution)/shard_map/all_to_all | solution.py:167
  96.7 1.7 shard_map.131
  98.4 23.5 %all_to_all.33 = bf16[4,8,4608]{2,1,0:T(8,128)(2,1)S(1)} all-to-all(bf16[4,8,4608]{2,1,0:T(8,128)(2,1)} %shard_map.131), channel_id=1, replica_groups=mesh['x'=4,'z_hi'=4,'core'=2,'z_lo'=4,'y'=8] {'z_hi'}, dimensions={0} | all-to-all | bytes 589824 | tf_op jit(solution)/shard_map/all_to_all | solution.py:167
  122.0 0.1 broadcast_in_dim.8
  122.0 14.0 %all_to_all.34 = bf16[4,32,4608]{2,1,0:T(8,128)(2,1)S(1)} all-to-all(bf16[4,32,4608]{2,1,0:T(8,128)(2,1)S(1)} %broadcast_in_dim.8), channel_id=1, replica_groups=mesh['x'=4,'z_hi'=4,'core'=2,'z_lo'=4,'y'=8] {'x'}, dimensions={0} | all-to-all | bytes 2359296 | tf_op jit(solution)/shard_map/all_to_all | solution.py:167
  136.1 0.0 copy-start
  136.1 1.9 %collective-permute-start.1 = (bf16[128,4608]{1,0:T(8,128)(2,1)S(1)}, bf16[128,4608]{1,0:T(8,128)(2,1)S(1)}, u32[]{:S(2)}, u32[]{:S(2)}) collective-permute-start(bf16[128,4608]{1,0:T(8,128)(2,1)S(1)} %bitcast.9), channel_id=1, source_target_pairs={{0,32},{32,0},{1,33},{33,1},{2,34},{34,2},{3,35},{35,3},{4,36},{36... | collective-permute-start | bytes 3538952 | tf_op jit(solution)/shard_map/ppermute | solution.py:250
  138.0 0.0 copy-done
  138.0 3.8 %shard_map.132.held_ref = bf16[32,2,8,192]{3,2,1,0:T(8,128)(2,1)} custom-call(s32[1]{0:T(128)} %bitcast.2.half_ref, bf16[128,4608]{1,0:T(8,128)(2,1)} %bitcast.10, bf16[1,192,1536]{2,1,0:T(8,128)(2,1)} %wg_ref.7, bf16[1,192,1536]{2,1,0:T(8,128)(2,1)} %wu_ref.7, bf16[1,192,1536]{2,1,0:T(8,128)(2,1)} %bitcast.14), custom_call_target="tpu_custom_call" | custom-call | tf_op jit(solution)/shard_map/pallas_call | solution.py:211
  141.8 0.0 collective-permute-done.1.other_ref
  141.8 0.0 copy-start.1
  141.8 1.0 copy-done.1
  142.8 5.2 %shard_map.133 = (bf16[32,2,8,192]{3,2,1,0:T(8,128)(2,1)}, bf16[1,192,1536]{2,1,0:T(8,128)(2,1)}, bf16[1,192,1536]{2,1,0:T(8,128)(2,1)}, bf16[1,192,1536]{2,1,0:T(8,128)(2,1)}) custom-call(s32[1]{0:T(128)} %bitcast.2.half_ref, bf16[128,4608]{1,0:T(8,128)(2,1)} %bitcast.11, bf16[128,4608]{1,0:T(8,128)(2,1)} %copy-done.1, ...), custom_call_target="tpu_custom_call", output_to_operand_aliasing={{0}: (8, {})} | custom-call | tf_op jit(solution)/shard_map/pallas_call | solution.py:211
  148.1 24.6 %all_to_all.35.back_ref = bf16[32,2,8,192]{3,2,1,0:T(8,128)(2,1)} all-to-all(bf16[32,2,8,192]{3,2,1,0:T(8,128)(2,1)} %get-tuple-element.15), channel_id=1, replica_groups=mesh['x'=4,'z_hi'=4,'core'=2,'z_lo'=4,'y'=8] {'z_lo','y'}, dimensions={0} | all-to-all | bytes 393216 | tf_op jit(solution)/shard_map/all_to_all | solution.py:167
  172.6 1.7 shard_map.134
Async XLA Ops:
  34.1 6.0 %collective-permute-start = (bf16[128,4608]{1,0:T(8,128)(2,1)}, bf16[128,4608]{1,0:T(8,128)(2,1)S(1)}, u32[]{:S(2)}, u32[]{:S(2)}) collective-permute-start(bf16[128,4608]{1,0:T(8,128)(2,1)} %shard_map.130), channel_id=1, source_target_pairs={{0,32},{32,0},{1,33},{33,1},{2,34},{34,2},{3,35},{35,3},{4,36},{36... | collective-permute-start | bytes 3538952 | tf_op jit(solution)/shard_map/ppermute | solution.py:239
  136.1 1.9 %copy-start = (bf16[4,32,4608]{2,1,0:T(8,128)(2,1)}, bf16[4,32,4608]{2,1,0:T(8,128)(2,1)S(1)}, u32[]{:S(2)}) copy-start(bf16[4,32,4608]{2,1,0:T(8,128)(2,1)S(1)} %all_to_all.34) | copy-start | bytes 3538948
  136.1 5.7 %collective-permute-start.1 = (bf16[128,4608]{1,0:T(8,128)(2,1)S(1)}, bf16[128,4608]{1,0:T(8,128)(2,1)S(1)}, u32[]{:S(2)}, u32[]{:S(2)}) collective-permute-start(bf16[128,4608]{1,0:T(8,128)(2,1)S(1)} %bitcast.9), channel_id=1, source_target_pairs={{0,32},{32,0},{1,33},{33,1},{2,34},{34,2},{3,35},{35,3},{4,36},{36... | collective-permute-start | bytes 3538952 | tf_op jit(solution)/shard_map/ppermute | solution.py:250
  141.8 1.0 copy-start.1

commit v3 on v2

v3 whole, which is shorter than its diff:
```python
import jax
import jax.numpy as jnp
from jax import lax
from jax.experimental import pallas as pl
from jax.experimental.pallas import tpu as pltpu
from jax.sharding import Mesh, PartitionSpec as P

EXPERTS = 4
TOP = 2
LIMIT = 8 * 2**20
TAIL_LIMIT = 16 * 2**20
INTERPRET = False
F32 = jnp.float32
LOW = jnp.bfloat16
NN = (((1,), (0,)), ((), ()))
NT = (((1,), (1,)), ((), ()))
TN = (((0,), (0,)), ((), ()))


def mm(a, b, dims):
    return lax.dot_general(a, b, dims, preferred_element_type=F32)


def column(values):
    spots = lax.broadcasted_iota(jnp.int32, (len(values), 1), 0)
    out = jnp.zeros((len(values), 1), F32)
    for t, value in enumerate(values):
        out = jnp.where(spots == t, value, out)
    return out


def expert_column(routes_ref, values, expert, count):
    picked = []
    for t in range(count):
        total = F32(0.0)
        for k in range(TOP):
            total = total + jnp.where(routes_ref[k, t] == expert, values(k, t), F32(0.0))
        picked.append(total)
    return column(picked)


def send_kernel(routes_ref, weights_ref, domains_ref, loss_ref, tok_ref, cot_ref, out_ref):
    count = tok_ref.shape[0]
    groups = out_ref.shape[0] // EXPERTS
    scale = column([loss_ref[domains_ref[t]] for t in range(count)])
    scaled = (cot_ref[...].astype(F32) * scale).astype(LOW).astype(F32)
    tok = tok_ref[...].astype(F32)
    for expert in range(EXPERTS):
        weight = expert_column(routes_ref, lambda k, t: weights_ref[k, t], expert, count)
        named = expert_column(routes_ref, lambda k, t: F32(1.0), expert, count)
        x_part = jnp.where(named > 0.0, tok, F32(0.0)).astype(LOW)
        g_part = (weight * scaled).astype(LOW)
        for group in range(groups):
            out_ref[expert * groups + group, 0] = x_part
            out_ref[expert * groups + group, 1] = g_part


def final_kernel(routes_ref, weights_ref, back_ref, mixed_ref, grad_ref):
    count = back_ref.shape[2]
    groups = back_ref.shape[0] // EXPERTS
    mixed, grad = None, None
    for expert in range(EXPERTS):
        weight = expert_column(routes_ref, lambda k, t: weights_ref[k, t], expert, count)
        out = back_ref[expert * groups, 0].astype(F32)
        inner = back_ref[expert * groups, 1].astype(F32)
        for group in range(1, groups):
            out = out + back_ref[expert * groups + group, 0].astype(F32)
            inner = inner + back_ref[expert * groups + group, 1].astype(F32)
        out = weight * out
        mixed = out if mixed is None else mixed + out
        grad = inner if grad is None else grad + inner
    mixed_ref[...] = mixed.astype(LOW)
    grad_ref[...] = grad.astype(LOW)


def rows_of(ref, half, which):
    blocks = ref.shape[0] // 2
    _, _, count, width = ref.shape
    return ref[pl.ds(half * blocks, blocks), which].reshape(blocks * count, width)


def partial_kernel(half_ref, got_ref, wg_ref, wu_ref, wd_ref, out_ref, bufs, sems):
    width = bufs.shape[2]
    half = half_ref[0]
    copies = []
    for i, weight_ref in enumerate((wg_ref, wu_ref, wd_ref)):
        copy = pltpu.make_async_copy(weight_ref.at[0], bufs.at[i], sems.at[i])
        copy.start()
        copies.append(copy)
    for i, copy in enumerate(copies):
        rows = rows_of(got_ref, half, 1 if i == 2 else 0)
        copy.wait()
        out_ref[:, i * width : (i + 1) * width] = mm(rows, bufs[i], NN).astype(LOW)


def middle_kernel(parts_ref, out_ref):
    copies, _, columns = parts_ref.shape
    width = columns // 3
    total = parts_ref[0].astype(F32)
    for i in range(1, copies):
        total = total + parts_ref[i].astype(F32)
    gate = total[:, :width]
    up = total[:, width : 2 * width]
    hidden_grad = total[:, 2 * width :]
    sigma = jax.nn.sigmoid(gate)
    hidden = (gate * sigma * up).astype(LOW)
    gate_grad = (hidden_grad * up * sigma * (1.0 + gate * (1.0 - sigma))).astype(LOW)
    up_grad = (hidden_grad * gate * sigma).astype(LOW)
    for i in range(copies):
        out_ref[i, :, :width] = hidden
        out_ref[i, :, width : 2 * width] = gate_grad
        out_ref[i, :, 2 * width :] = up_grad


def row_products(act_ref, wg_ref, wu_ref, wd_ref):
    width = wg_ref.shape[2]
    out = mm(act_ref[:, :width], wd_ref[0], NT)
    inner = mm(act_ref[:, width : 2 * width], wg_ref[0], NT)
    return out, inner + mm(act_ref[:, 2 * width :], wu_ref[0], NT)


def own_kernel(act_ref, wg_ref, wu_ref, wd_ref, back_ref):
    blocks, _, count, width = back_ref.shape
    out, inner = row_products(act_ref, wg_ref, wu_ref, wd_ref)
    back_ref[:, 0] = out.reshape(blocks, count, width).astype(LOW)
    back_ref[:, 1] = inner.reshape(blocks, count, width).astype(LOW)


def tail_kernel(
    half_ref,
    own_ref,
    other_ref,
    got_ref,
    held_ref,
    wg_ref,
    wu_ref,
    wd_ref,
    back_ref,
    gg_ref,
    gu_ref,
    gd_ref,
    gg_buf,
    gu_buf,
    gd_buf,
    sems,
):
    width = wg_ref.shape[2]
    blocks, _, count, rows_width = held_ref.shape
    half = half_ref[0]
    act = jnp.concatenate([own_ref[...], other_ref[...]], axis=0)
    copies = []
    for i, (which, buf, dst) in enumerate(
        ((1, gd_buf, gd_ref), (0, gg_buf, gg_ref), (0, gu_buf, gu_ref))
    ):
        rows = [rows_of(got_ref, half, which), rows_of(got_ref, 1 - half, which)]
        rows = jnp.concatenate(rows, axis=0)
        buf[0] = mm(rows, act[:, i * width : (i + 1) * width], TN).astype(LOW)
        copy = pltpu.make_async_copy(buf, dst, sems.at[i])
        copy.start()
        copies.append(copy)
    out, inner = row_products(other_ref, wg_ref, wu_ref, wd_ref)
    back_ref[pl.ds(half * blocks, blocks)] = held_ref[...]
    other = pl.ds((1 - half) * blocks, blocks)
    back_ref[other, 0] = out.reshape(blocks, count, rows_width).astype(LOW)
    back_ref[other, 1] = inner.reshape(blocks, count, rows_width).astype(LOW)
    for copy in copies:
        copy.wait()


def near(value):
    return value if INTERPRET else pltpu.with_memory_space_constraint(value, pltpu.VMEM)


def far(value):
    return value if INTERPRET else pltpu.with_memory_space_constraint(value, pltpu.HBM)


def near_out(shape):
    return jax.ShapeDtypeStruct(shape, LOW) if INTERPRET else pltpu.VMEM(shape, LOW)


def call(kernel, in_specs, out_specs, shapes, args, limit, scratch=()):
    return pl.pallas_call(
        kernel,
        out_shape=shapes,
        in_specs=in_specs,
        out_specs=out_specs,
        scratch_shapes=scratch,
        compiler_params=pltpu.CompilerParams(vmem_limit_bytes=limit),
        interpret=INTERPRET,
    )(*args)


def exchange(value, axis):
    return lax.all_to_all(value, axis, split_axis=0, concat_axis=0, tiled=True)


def per_device(
    tokens, cotangent, routes, route_weights, domains, loss_weights, w_gate, w_up, w_down
):
    tok_count, local_width = tokens.shape
    n_x, n_z, n_core = lax.axis_size("x"), lax.axis_size("z_hi"), lax.axis_size("core")
    owners = EXPERTS * lax.axis_size("y")
    grp_width = w_gate.shape[2]
    columns = 3 * grp_width
    half_rows = owners * tok_count // n_core
    routes_t = routes.T
    weights_t = route_weights.T
    half = lax.axis_index("core").reshape(1).astype(jnp.int32)
    swap = [(0, 1), (1, 0)]
    plain_weights = (w_gate, w_up, jnp.swapaxes(w_down, 1, 2))
    far_weights = [far(w) for w in plain_weights]
    weights = [near(w) for w in plain_weights]

    smem = pl.BlockSpec(memory_space=pltpu.SMEM)
    vmem = pl.BlockSpec(memory_space=pltpu.VMEM)
    hbm = pl.BlockSpec(memory_space=pl.ANY)
    block = (owners, 2, tok_count, local_width)
    send = call(
        send_kernel,
        [smem] * 4 + [vmem] * 2,
        vmem,
        jax.ShapeDtypeStruct(block, LOW),
        (routes_t, weights_t, domains, loss_weights, tokens, cotangent),
        None,
    )
    send, half, rest = lax.optimization_barrier((send, half, 1 - half))
    got = near(exchange(send, ("z_lo", "y")))

    def partial(which):
        return call(
            partial_kernel,
            [smem, vmem] + [pl.BlockSpec(memory_space=pl.ANY if INTERPRET else pltpu.HBM)] * 3,
            vmem,
            near_out((half_rows, columns)),
            (which, got, *far_weights),
            LIMIT,
            [
                pltpu.VMEM((3, local_width, grp_width), LOW),
                pltpu.SemaphoreType.DMA((3,)),
            ],
        )

    arrived = lax.ppermute(partial(rest), "core", swap)
    sums = (partial(half).astype(F32) + arrived.astype(F32)).astype(LOW)
    parts = exchange(sums.reshape(n_x, half_rows // n_x, columns), "x")
    sums = jnp.sum(parts.astype(F32), axis=0).astype(LOW)
    parts = exchange(sums.reshape(n_z, sums.shape[0] // n_z, columns), "z_hi")
    copies = call(middle_kernel, [vmem], vmem, near_out(parts.shape), (near(parts),), LIMIT)
    act = exchange(copies, "z_hi").reshape(1, half_rows // n_x, columns)
    act = exchange(jnp.broadcast_to(act, (n_x,) + act.shape[1:]), "x")
    own = act.reshape(half_rows, columns)
    other = lax.ppermute(own, "core", swap)
    own = near(own)
    held = call(
        own_kernel,
        [vmem] * 4,
        vmem,
        near_out((owners // n_core,) + block[1:]),
        (own, *weights),
        LIMIT,
    )
    grad = jax.ShapeDtypeStruct((1, local_width, grp_width), LOW)
    buf = pltpu.VMEM((1, local_width, grp_width), LOW)
    back, grad_gate, grad_up, grad_down = call(
        tail_kernel,
        [smem] + [vmem] * 7,
        (vmem, hbm, hbm, hbm),
        (near_out(block), grad, grad, grad),
        (half, own, near(other), got, held, *weights),
        TAIL_LIMIT,
        [buf, buf, buf, pltpu.SemaphoreType.DMA((3,))],
    )
    back = exchange(back, ("z_lo", "y"))
    flat = jax.ShapeDtypeStruct((tok_count, local_width), LOW)
    mixed, grad_tokens = call(
        final_kernel,
        [smem, smem, vmem],
        (vmem, vmem),
        (flat, flat),
        (routes_t, weights_t, near(back)),
        LIMIT,
    )
    return mixed, grad_tokens, grad_gate, grad_up, jnp.swapaxes(grad_down, 1, 2)


def solution(mesh):
    n_fsdp, n_expert = mesh.shape["fsdp"], mesh.shape["expert"]
    n_x = 4 if n_fsdp >= 32 else 2
    split = (n_x, n_fsdp // (2 * n_x), 2, EXPERTS, n_expert // EXPERTS)
    fine = Mesh(mesh.devices.reshape(split), ("x", "z_hi", "core", "z_lo", "y"))
    fsdp, expert = ("x", "z_hi", "core"), ("z_lo", "y")
    in_specs = (
        P(expert, fsdp),
        P(expert, fsdp),
        P(expert, None),
        P(expert, None),
        P(expert),
        P(),
        P(expert, fsdp, None),
        P(expert, fsdp, None),
        P(expert, None, fsdp),
    )
    out_specs = (
        P(expert, fsdp),
        P(expert, fsdp),
        P(expert, fsdp, None),
        P(expert, fsdp, None),
        P(expert, None, fsdp),
    )
    return jax.shard_map(
        per_device, mesh=fine, in_specs=in_specs, out_specs=out_specs, check_vma=False
    )
```

time: 175 us -> 161 us (0.920)
  Pallas kernels: 22 us -> 9.6 us
  blocking collectives: 145 us -> 142 us
  waiting for transfers between devices: 0.01 us -> 2.96 us
    pallas_call x7, Pallas kernels: 22 us -> 9.6 us  [call(): pl.pallas_call(kernel, out_shape=shapes, in_specs=in_specs, out_specs=out...]
    all_to_all x6, blocking collectives: 145 us -> 142 us  [exchange(): return lax.all_to_all(value, axis, split_axis=0, concat_axis=0, tiled=True)]
    ppermute x1, waiting for transfers between devices: 0.01 us -> 2.04 us  [per_device(): other = lax.ppermute(own, 'core', swap)]
  transfers between devices with their start and end apart: 2 -> 2, of which waited for: 0 -> 2; matrix products, arithmetic and copies ran while one was open for 0% -> 0% of each run, Pallas kernels for 4% -> 2%
where the time goes in v3:
time: 161 us; the launch traced here: 160 us
  blocking collectives  142 us (88%)
  Pallas kernels  9.6 us (6%)
  starting transfers between devices  3.83 us (2%)
  waiting for transfers between devices  2.96 us (2%)
    all_to_all x6, blocking collectives, exchange(): return lax.all_to_all(value, axis, split_axis=0, concat_axis=0, tiled=True)  142 us
    pallas_call x7, Pallas kernels, call(): pl.pallas_call(kernel, out_shape=shapes, in_specs=in_specs, out_specs=out...  9.6 us
  transfers between devices with their start and end apart: 2, of which 2 were waited for; matrix products, arithmetic and copies ran while one was open for 0% of the time, Pallas kernels for 2%

profile of v3, /device:TPU:8, one launch (start us, length us, event | category | flops | bytes accessed | tf_op | source)
XLA Modules:
  0.0 160.2 jit_solution(8526307415509469512)
XLA Ops:
  0.6 1.6 shard_map.128
  2.2 27.2 %all_to_all.30.got_ref = bf16[32,2,8,192]{3,2,1,0:T(8,128)(2,1)S(1)} all-to-all(bf16[32,2,8,192]{3,2,1,0:T(8,128)(2,1)} %shard_map.128), channel_id=1, replica_groups=mesh['x'=4,'z_hi'=4,'core'=2,'z_lo'=4,'y'=8] {'z_lo','y'}, dimensions={0} | all-to-all | bytes 393216 | tf_op jit(solution)/shard_map/all_to_all | solution.py:195
  29.4 1.9 %shard_map.130 = bf16[128,4608]{1,0:T(8,128)(2,1)S(1)} custom-call(s32[1]{0:T(128)S(6)} %sub.3.half_ref, bf16[32,2,8,192]{3,2,1,0:T(8,128)(2,1)S(1)} %all_to_all.30.got_ref, bf16[1,192,1536]{2,1,0:T(8,128)(2,1)} %wg_ref.7, bf16[1,192,1536]{2,1,0:T(8,128)(2,1)} %wu_ref.7, bf16[1,192,1536]{2,1,0:T(8,128)(2,1)} %bitcast.12), custom_call_target="tpu_custom_call" | custom-call | tf_op jit(solution)/shard_map/pallas_call | solution.py:183
  31.3 1.9 %collective-permute-start = (bf16[128,4608]{1,0:T(8,128)(2,1)S(1)}, bf16[128,4608]{1,0:T(8,128)(2,1)S(1)}, u32[]{:S(2)}, u32[]{:S(2)}) collective-permute-start(bf16[128,4608]{1,0:T(8,128)(2,1)S(1)} %shard_map.130), channel_id=1, source_target_pairs={{0,32},{32,0},{1,33},{33,1},{2,34},{34,2},{3,35},{35,3},{4,36},{36... | collective-permute-start | bytes 3538952 | tf_op jit(solution)/shard_map/ppermute | solution.py:244
  33.2 1.9 %shard_map.129 = bf16[128,4608]{1,0:T(8,128)(2,1)S(1)} custom-call(s32[1]{0:T(128)} %bitcast.2.half_ref, bf16[32,2,8,192]{3,2,1,0:T(8,128)(2,1)S(1)} %all_to_all.30.got_ref, bf16[1,192,1536]{2,1,0:T(8,128)(2,1)} %wg_ref.7, bf16[1,192,1536]{2,1,0:T(8,128)(2,1)} %wu_ref.7, bf16[1,192,1536]{2,1,0:T(8,128)(2,1)} %bitcast.13), custom_call_target="tpu_custom_call" | custom-call | tf_op jit(solution)/shard_map/pallas_call | solution.py:183
  35.1 0.9 collective-permute-done
  36.0 0.3 add_convert_fusion
  36.3 19.5 %all_to_all.31 = bf16[4,32,4608]{2,1,0:T(8,128)(2,1)S(1)} all-to-all(bf16[4,32,4608]{2,1,0:T(8,128)(2,1)S(1)} %bitcast.20), channel_id=1, replica_groups=mesh['x'=4,'z_hi'=4,'core'=2,'z_lo'=4,'y'=8] {'x'}, dimensions={0} | all-to-all | bytes 2359296 | tf_op jit(solution)/shard_map/all_to_all | solution.py:195
  55.8 0.3 reduce_sum.12
  56.1 35.2 %all_to_all.32.parts_ref = bf16[4,8,4608]{2,1,0:T(8,128)(2,1)S(1)} all-to-all(bf16[4,8,4608]{2,1,0:T(8,128)(2,1)S(1)} %bitcast.21), channel_id=1, replica_groups=mesh['x'=4,'z_hi'=4,'core'=2,'z_lo'=4,'y'=8] {'z_hi'}, dimensions={0} | all-to-all | bytes 589824 | tf_op jit(solution)/shard_map/all_to_all | solution.py:195
  91.3 0.1 shard_map.131
  91.3 24.2 %all_to_all.33 = bf16[4,8,4608]{2,1,0:T(8,128)(2,1)S(1)} all-to-all(bf16[4,8,4608]{2,1,0:T(8,128)(2,1)S(1)} %shard_map.131), channel_id=1, replica_groups=mesh['x'=4,'z_hi'=4,'core'=2,'z_lo'=4,'y'=8] {'z_hi'}, dimensions={0} | all-to-all | bytes 589824 | tf_op jit(solution)/shard_map/all_to_all | solution.py:195
  115.5 0.1 broadcast_in_dim.8
  115.6 0.0 copy-start
  115.6 0.0 copy-start.1
  115.7 0.0 copy-start.2
  115.7 15.4 %all_to_all.34 = bf16[4,32,4608]{2,1,0:T(8,128)(2,1)S(1)} all-to-all(bf16[4,32,4608]{2,1,0:T(8,128)(2,1)S(1)} %broadcast_in_dim.8), channel_id=1, replica_groups=mesh['x'=4,'z_hi'=4,'core'=2,'z_lo'=4,'y'=8] {'x'}, dimensions={0} | all-to-all | bytes 2359296 | tf_op jit(solution)/shard_map/all_to_all | solution.py:195
  131.1 1.9 %collective-permute-start.1 = (bf16[128,4608]{1,0:T(8,128)(2,1)S(1)}, bf16[128,4608]{1,0:T(8,128)(2,1)S(1)}, u32[]{:S(2)}, u32[]{:S(2)}) collective-permute-start(bf16[128,4608]{1,0:T(8,128)(2,1)S(1)} %bitcast.9), channel_id=1, source_target_pairs={{0,32},{32,0},{1,33},{33,1},{2,34},{34,2},{3,35},{35,3},{4,36},{36... | collective-permute-start | bytes 3538952 | tf_op jit(solution)/shard_map/ppermute | solution.py:253
  133.0 0.0 copy-done
  133.0 0.0 copy-done.1
  133.0 0.0 copy-done.2
  133.0 0.7 shard_map.132.held_ref
  133.7 0.0 copy-start.3
  133.7 0.0 copy-start.4
  133.8 2.0 %collective-permute-done.1.other_ref = bf16[128,4608]{1,0:T(8,128)(2,1)S(1)} collective-permute-done((bf16[128,4608]{1,0:T(8,128)(2,1)S(1)}, bf16[128,4608]{1,0:T(8,128)(2,1)S(1)}, u32[]{:S(2)}, u32[]{:S(2)}) %collective-permute-start.1) | collective-permute-done | bytes 1179680 | tf_op jit(solution)/shard_map/ppermute | solution.py:253
  135.8 2.2 %shard_map.133 = (bf16[32,2,8,192]{3,2,1,0:T(8,128)(2,1)S(1)}, bf16[1,192,1536]{2,1,0:T(8,128)(2,1)}, bf16[1,192,1536]{2,1,0:T(8,128)(2,1)}, bf16[1,192,1536]{2,1,0:T(8,128)(2,1)}) custom-call(s32[1]{0:T(128)} %bitcast.2.half_ref, bf16[128,4608]{1,0:T(8,128)(2,1)S(1)} %bitcast.11, bf16[128,4608]{1,0:T(8,128)(2,1)S(1)} %collective-permute-done.1.other_ref, ...), custom_call_target="tpu_custom_call" | custom-call | tf_op jit(solution)/shard_map/pallas_call | solution.py:183
  138.0 20.9 %all_to_all.35.back_ref = bf16[32,2,8,192]{3,2,1,0:T(8,128)(2,1)S(1)} all-to-all(bf16[32,2,8,192]{3,2,1,0:T(8,128)(2,1)S(1)} %get-tuple-element.17), channel_id=1, replica_groups=mesh['x'=4,'z_hi'=4,'core'=2,'z_lo'=4,'y'=8] {'z_lo','y'}, dimensions={0} | all-to-all | bytes 393216 | tf_op jit(solution)/shard_map/all_to_all | solution.py:195
  158.9 0.0 copy-done.3
  158.9 0.0 copy-done.4
  159.0 1.3 shard_map.134
Async XLA Ops:
  31.3 4.7 %collective-permute-start = (bf16[128,4608]{1,0:T(8,128)(2,1)S(1)}, bf16[128,4608]{1,0:T(8,128)(2,1)S(1)}, u32[]{:S(2)}, u32[]{:S(2)}) collective-permute-start(bf16[128,4608]{1,0:T(8,128)(2,1)S(1)} %shard_map.130), channel_id=1, source_target_pairs={{0,32},{32,0},{1,33},{33,1},{2,34},{34,2},{3,35},{35,3},{4,36},{36... | collective-permute-start | bytes 3538952 | tf_op jit(solution)/shard_map/ppermute | solution.py:244
  115.6 17.4 %copy-start = (bf16[1,192,1536]{2,1,0:T(8,128)(2,1)S(1)}, bf16[1,192,1536]{2,1,0:T(8,128)(2,1)}, u32[]{:S(2)}) copy-start(bf16[1,192,1536]{2,1,0:T(8,128)(2,1)} %wg_ref.7) | copy-start | bytes 1769476
  115.6 17.4 %copy-start.1 = (bf16[1,192,1536]{2,1,0:T(8,128)(2,1)S(1)}, bf16[1,192,1536]{2,1,0:T(8,128)(2,1)}, u32[]{:S(2)}) copy-start(bf16[1,192,1536]{2,1,0:T(8,128)(2,1)} %wu_ref.7) | copy-start | bytes 1769476
  115.7 17.4 %copy-start.2 = (bf16[1,1536,192]{1,2,0:T(8,128)(2,1)S(1)}, bf16[1,1536,192]{1,2,0:T(8,128)(2,1)}, u32[]{:S(2)}) copy-start(bf16[1,1536,192]{1,2,0:T(8,128)(2,1)} %param.17) | copy-start | bytes 1769476
  131.1 4.7 %collective-permute-start.1 = (bf16[128,4608]{1,0:T(8,128)(2,1)S(1)}, bf16[128,4608]{1,0:T(8,128)(2,1)S(1)}, u32[]{:S(2)}, u32[]{:S(2)}) collective-permute-start(bf16[128,4608]{1,0:T(8,128)(2,1)S(1)} %bitcast.9), channel_id=1, source_target_pairs={{0,32},{32,0},{1,33},{33,1},{2,34},{34,2},{3,35},{35,3},{4,36},{36... | collective-permute-start | bytes 3538952 | tf_op jit(solution)/shard_map/ppermute | solution.py:253
  133.7 25.2 %copy-start.3 = (s32[8,2]{0,1:T(2,128)S(1)}, s32[8,2]{0,1:T(2,128)}, u32[]{:S(2)}) copy-start(s32[8,2]{0,1:T(2,128)} %param.11) | copy-start | bytes 196
  133.7 25.2 %copy-start.4 = (f32[8,2]{0,1:T(2,128)S(1)}, f32[8,2]{0,1:T(2,128)}, u32[]{:S(2)}) copy-start(f32[8,2]{0,1:T(2,128)} %param.12) | copy-start | bytes 196

commit v4 on v3

--- a/solution.py
+++ b/solution.py
@@ -48,35 +48,33 @@
     for expert in range(EXPERTS):
         weight = expert_column(routes_ref, lambda k, t: weights_ref[k, t], expert, count)
         named = expert_column(routes_ref, lambda k, t: F32(1.0), expert, count)
-        x_part = jnp.where(named > 0.0, tok, F32(0.0)).astype(LOW)
-        g_part = (weight * scaled).astype(LOW)
+        x_part = jnp.where(named > 0.0, tok, F32(0.0))
+        g_part = weight * scaled
+        both = jnp.concatenate([x_part, g_part], axis=1).astype(LOW)
         for group in range(groups):
-            out_ref[expert * groups + group, 0] = x_part
-            out_ref[expert * groups + group, 1] = g_part
+            out_ref[expert * groups + group] = both
 
 
 def final_kernel(routes_ref, weights_ref, back_ref, mixed_ref, grad_ref):
-    count = back_ref.shape[2]
+    count, width = mixed_ref.shape
     groups = back_ref.shape[0] // EXPERTS
     mixed, grad = None, None
     for expert in range(EXPERTS):
         weight = expert_column(routes_ref, lambda k, t: weights_ref[k, t], expert, count)
-        out = back_ref[expert * groups, 0].astype(F32)
-        inner = back_ref[expert * groups, 1].astype(F32)
+        total = back_ref[expert * groups].astype(F32)
         for group in range(1, groups):
-            out = out + back_ref[expert * groups + group, 0].astype(F32)
-            inner = inner + back_ref[expert * groups + group, 1].astype(F32)
-        out = weight * out
+            total = total + back_ref[expert * groups + group].astype(F32)
+        out = weight * total
         mixed = out if mixed is None else mixed + out
-        grad = inner if grad is None else grad + inner
-    mixed_ref[...] = mixed.astype(LOW)
-    grad_ref[...] = grad.astype(LOW)
-
-
-def rows_of(ref, half, which):
-    blocks = ref.shape[0] // 2
-    _, _, count, width = ref.shape
-    return ref[pl.ds(half * blocks, blocks), which].reshape(blocks * count, width)
+        grad = total if grad is None else grad + total
+    mixed_ref[...] = mixed[:, :width].astype(LOW)
+    grad_ref[...] = grad[:, width:].astype(LOW)
+
+
+def rows_of(ref, half):
+    blocks, count, width = ref.shape
+    blocks = blocks // 2
+    return ref[pl.ds(half * blocks, blocks)].reshape(blocks * count, width)
 
 
 def partial_kernel(half_ref, got_ref, wg_ref, wu_ref, wd_ref, out_ref, bufs, sems):
@@ -87,8 +85,10 @@
         copy = pltpu.make_async_copy(weight_ref.at[0], bufs.at[i], sems.at[i])
         copy.start()
         copies.append(copy)
+    both = rows_of(got_ref, half)
+    depth = bufs.shape[1]
     for i, copy in enumerate(copies):
-        rows = rows_of(got_ref, half, 1 if i == 2 else 0)
+        rows = both[:, depth:] if i == 2 else both[:, :depth]
         copy.wait()
         out_ref[:, i * width : (i + 1) * width] = mm(rows, bufs[i], NN).astype(LOW)
 
@@ -116,14 +116,12 @@
     width = wg_ref.shape[2]
     out = mm(act_ref[:, :width], wd_ref[0], NT)
     inner = mm(act_ref[:, width : 2 * width], wg_ref[0], NT)
-    return out, inner + mm(act_ref[:, 2 * width :], wu_ref[0], NT)
+    inner = inner + mm(act_ref[:, 2 * width :], wu_ref[0], NT)
+    return jnp.concatenate([out, inner], axis=1).astype(LOW)
 
 
 def own_kernel(act_ref, wg_ref, wu_ref, wd_ref, back_ref):
-    blocks, _, count, width = back_ref.shape
-    out, inner = row_products(act_ref, wg_ref, wu_ref, wd_ref)
-    back_ref[:, 0] = out.reshape(blocks, count, width).astype(LOW)
-    back_ref[:, 1] = inner.reshape(blocks, count, width).astype(LOW)
+    back_ref[...] = row_products(act_ref, wg_ref, wu_ref, wd_ref).reshape(back_ref.shape)
 
 
 def tail_kernel(
@@ -145,24 +143,21 @@
     sems,
 ):
     width = wg_ref.shape[2]
-    blocks, _, count, rows_width = held_ref.shape
+    blocks = held_ref.shape[0]
     half = half_ref[0]
     act = jnp.concatenate([own_ref[...], other_ref[...]], axis=0)
+    both = jnp.concatenate([rows_of(got_ref, half), rows_of(got_ref, 1 - half)], axis=0)
+    depth = both.shape[1] // 2
     copies = []
-    for i, (which, buf, dst) in enumerate(
-        ((1, gd_buf, gd_ref), (0, gg_buf, gg_ref), (0, gu_buf, gu_ref))
-    ):
-        rows = [rows_of(got_ref, half, which), rows_of(got_ref, 1 - half, which)]
-        rows = jnp.concatenate(rows, axis=0)
+    for i, (buf, dst) in enumerate(((gd_buf, gd_ref), (gg_buf, gg_ref), (gu_buf, gu_ref))):
+        rows = both[:, :depth] if i else both[:, depth:]
         buf[0] = mm(rows, act[:, i * width : (i + 1) * width], TN).astype(LOW)
         copy = pltpu.make_async_copy(buf, dst, sems.at[i])
         copy.start()
         copies.append(copy)
-    out, inner = row_products(other_ref, wg_ref, wu_ref, wd_ref)
+    rows = row_products(other_ref, wg_ref, wu_ref, wd_ref)
     back_ref[pl.ds(half * blocks, blocks)] = held_ref[...]
-    other = pl.ds((1 - half) * blocks, blocks)
-    back_ref[other, 0] = out.reshape(blocks, count, rows_width).astype(LOW)
-    back_ref[other, 1] = inner.reshape(blocks, count, rows_width).astype(LOW)
+    back_ref[pl.ds((1 - half) * blocks, blocks)] = rows.reshape(held_ref.shape)
     for copy in copies:
         copy.wait()
 
@@ -215,12 +210,12 @@
     smem = pl.BlockSpec(memory_space=pltpu.SMEM)
     vmem = pl.BlockSpec(memory_space=pltpu.VMEM)
     hbm = pl.BlockSpec(memory_space=pl.ANY)
-    block = (owners, 2, tok_count, local_width)
+    block = (owners, tok_count, 2 * local_width)
     send = call(
         send_kernel,
         [smem] * 4 + [vmem] * 2,
         vmem,
-        jax.ShapeDtypeStruct(block, LOW),
+        near_out(block),
         (routes_t, weights_t, domains, loss_weights, tokens, cotangent),
         None,
     )

time: 161 us -> 157 us (0.975)
  blocking collectives: 142 us -> 139 us
    all_to_all x6, blocking collectives: 142 us -> 139 us  [exchange(): return lax.all_to_all(value, axis, split_axis=0, concat_axis=0, tiled=True)]
where the time goes in v4:
time: 157 us
  blocking collectives  139 us (89%)
  Pallas kernels  9.23 us (6%)
  starting transfers between devices  3.83 us (2%)
  waiting for transfers between devices  2.84 us (2%)
    all_to_all x6, blocking collectives, exchange(): return lax.all_to_all(value, axis, split_axis=0, concat_axis=0, tiled=True)  139 us
    pallas_call x7, Pallas kernels, call(): pl.pallas_call(kernel, out_shape=shapes, in_specs=in_specs, out_specs=out...  9.23 us
  transfers between devices with their start and end apart: 2, of which 2 were waited for; matrix products, arithmetic and copies ran while one was open for 0% of the time, Pallas kernels for 2%

profile of v4, /device:TPU:8, one launch (start us, length us, event | category | flops | bytes accessed | tf_op | source)
XLA Modules:
  0.0 156.7 jit_solution(2355868112649942345)
XLA Ops:
  0.6 0.9 shard_map.128
  1.5 25.9 %all_to_all.30.got_ref = bf16[32,8,384]{2,1,0:T(8,128)(2,1)S(1)} all-to-all(bf16[32,8,384]{2,1,0:T(8,128)(2,1)S(1)} %shard_map.128), channel_id=1, replica_groups=mesh['x'=4,'z_hi'=4,'core'=2,'z_lo'=4,'y'=8] {'z_lo','y'}, dimensions={0} | all-to-all | bytes 393216 | tf_op jit(solution)/shard_map/all_to_all | solution.py:190
  27.4 1.9 %shard_map.130 = bf16[128,4608]{1,0:T(8,128)(2,1)S(1)} custom-call(s32[1]{0:T(128)S(6)} %sub.3.half_ref, bf16[32,8,384]{2,1,0:T(8,128)(2,1)S(1)} %all_to_all.30.got_ref, bf16[1,192,1536]{2,1,0:T(8,128)(2,1)} %wg_ref.7, bf16[1,192,1536]{2,1,0:T(8,128)(2,1)} %wu_ref.7, bf16[1,192,1536]{2,1,0:T(8,128)(2,1)} %bitcast.12), custom_call_target="tpu_custom_call" | custom-call | tf_op jit(solution)/shard_map/pallas_call | solution.py:178
  29.4 1.9 %collective-permute-start = (bf16[128,4608]{1,0:T(8,128)(2,1)S(1)}, bf16[128,4608]{1,0:T(8,128)(2,1)S(1)}, u32[]{:S(2)}, u32[]{:S(2)}) collective-permute-start(bf16[128,4608]{1,0:T(8,128)(2,1)S(1)} %shard_map.130), channel_id=1, source_target_pairs={{0,32},{32,0},{1,33},{33,1},{2,34},{34,2},{3,35},{35,3},{4,36},{36... | collective-permute-start | bytes 3538952 | tf_op jit(solution)/shard_map/ppermute | solution.py:239
  31.3 1.9 %shard_map.129 = bf16[128,4608]{1,0:T(8,128)(2,1)S(1)} custom-call(s32[1]{0:T(128)} %bitcast.2.half_ref, bf16[32,8,384]{2,1,0:T(8,128)(2,1)S(1)} %all_to_all.30.got_ref, bf16[1,192,1536]{2,1,0:T(8,128)(2,1)} %wg_ref.7, bf16[1,192,1536]{2,1,0:T(8,128)(2,1)} %wu_ref.7, bf16[1,192,1536]{2,1,0:T(8,128)(2,1)} %bitcast.13), custom_call_target="tpu_custom_call" | custom-call | tf_op jit(solution)/shard_map/pallas_call | solution.py:178
  33.2 0.9 collective-permute-done
  34.1 0.3 add_convert_fusion
  34.4 19.5 %all_to_all.31 = bf16[4,32,4608]{2,1,0:T(8,128)(2,1)S(1)} all-to-all(bf16[4,32,4608]{2,1,0:T(8,128)(2,1)S(1)} %bitcast.20), channel_id=1, replica_groups=mesh['x'=4,'z_hi'=4,'core'=2,'z_lo'=4,'y'=8] {'x'}, dimensions={0} | all-to-all | bytes 2359296 | tf_op jit(solution)/shard_map/all_to_all | solution.py:190
  53.9 0.3 reduce_sum.12
  54.2 34.9 %all_to_all.32.parts_ref = bf16[4,8,4608]{2,1,0:T(8,128)(2,1)S(1)} all-to-all(bf16[4,8,4608]{2,1,0:T(8,128)(2,1)S(1)} %bitcast.21), channel_id=1, replica_groups=mesh['x'=4,'z_hi'=4,'core'=2,'z_lo'=4,'y'=8] {'z_hi'}, dimensions={0} | all-to-all | bytes 589824 | tf_op jit(solution)/shard_map/all_to_all | solution.py:190
  89.1 0.1 shard_map.131
  89.2 23.7 %all_to_all.33 = bf16[4,8,4608]{2,1,0:T(8,128)(2,1)S(1)} all-to-all(bf16[4,8,4608]{2,1,0:T(8,128)(2,1)S(1)} %shard_map.131), channel_id=1, replica_groups=mesh['x'=4,'z_hi'=4,'core'=2,'z_lo'=4,'y'=8] {'z_hi'}, dimensions={0} | all-to-all | bytes 589824 | tf_op jit(solution)/shard_map/all_to_all | solution.py:190
  112.8 0.1 broadcast_in_dim.8
  112.9 0.0 copy-start
  112.9 0.0 copy-start.1
  112.9 0.0 copy-start.2
  112.9 14.2 %all_to_all.34 = bf16[4,32,4608]{2,1,0:T(8,128)(2,1)S(1)} all-to-all(bf16[4,32,4608]{2,1,0:T(8,128)(2,1)S(1)} %broadcast_in_dim.8), channel_id=1, replica_groups=mesh['x'=4,'z_hi'=4,'core'=2,'z_lo'=4,'y'=8] {'x'}, dimensions={0} | all-to-all | bytes 2359296 | tf_op jit(solution)/shard_map/all_to_all | solution.py:190
  127.1 1.9 %collective-permute-start.1 = (bf16[128,4608]{1,0:T(8,128)(2,1)S(1)}, bf16[128,4608]{1,0:T(8,128)(2,1)S(1)}, u32[]{:S(2)}, u32[]{:S(2)}) collective-permute-start(bf16[128,4608]{1,0:T(8,128)(2,1)S(1)} %bitcast.9), channel_id=1, source_target_pairs={{0,32},{32,0},{1,33},{33,1},{2,34},{34,2},{3,35},{35,3},{4,36},{36... | collective-permute-start | bytes 3538952 | tf_op jit(solution)/shard_map/ppermute | solution.py:248
  129.0 0.0 copy-done
  129.0 0.0 copy-done.1
  129.0 0.0 copy-done.2
  129.0 0.8 shard_map.132.held_ref
  129.8 0.0 copy-start.3
  129.8 0.0 copy-start.4
  129.9 2.0 %collective-permute-done.1.other_ref = bf16[128,4608]{1,0:T(8,128)(2,1)S(1)} collective-permute-done((bf16[128,4608]{1,0:T(8,128)(2,1)S(1)}, bf16[128,4608]{1,0:T(8,128)(2,1)S(1)}, u32[]{:S(2)}, u32[]{:S(2)}) %collective-permute-start.1) | collective-permute-done | bytes 1179680 | tf_op jit(solution)/shard_map/ppermute | solution.py:248
  131.8 2.3 %shard_map.133 = (bf16[32,8,384]{2,1,0:T(8,128)(2,1)S(1)}, bf16[1,192,1536]{2,1,0:T(8,128)(2,1)}, bf16[1,192,1536]{2,1,0:T(8,128)(2,1)}, bf16[1,192,1536]{2,1,0:T(8,128)(2,1)}) custom-call(s32[1]{0:T(128)} %bitcast.2.half_ref, bf16[128,4608]{1,0:T(8,128)(2,1)S(1)} %bitcast.11, bf16[128,4608]{1,0:T(8,128)(2,1)S(1)} %collective-permute-done.1.other_ref, ...), custom_call_target="tpu_custom_call" | custom-call | tf_op jit(solution)/shard_map/pallas_call | solution.py:178
  134.1 21.2 %all_to_all.35.back_ref = bf16[32,8,384]{2,1,0:T(8,128)(2,1)S(1)} all-to-all(bf16[32,8,384]{2,1,0:T(8,128)(2,1)S(1)} %get-tuple-element.17), channel_id=1, replica_groups=mesh['x'=4,'z_hi'=4,'core'=2,'z_lo'=4,'y'=8] {'z_lo','y'}, dimensions={0} | all-to-all | bytes 393216 | tf_op jit(solution)/shard_map/all_to_all | solution.py:190
  155.4 0.0 copy-done.3
  155.4 0.0 copy-done.4
  155.4 1.3 shard_map.134
Async XLA Ops:
  29.4 4.7 %collective-permute-start = (bf16[128,4608]{1,0:T(8,128)(2,1)S(1)}, bf16[128,4608]{1,0:T(8,128)(2,1)S(1)}, u32[]{:S(2)}, u32[]{:S(2)}) collective-permute-start(bf16[128,4608]{1,0:T(8,128)(2,1)S(1)} %shard_map.130), channel_id=1, source_target_pairs={{0,32},{32,0},{1,33},{33,1},{2,34},{34,2},{3,35},{35,3},{4,36},{36... | collective-permute-start | bytes 3538952 | tf_op jit(solution)/shard_map/ppermute | solution.py:239
  112.9 16.1 %copy-start = (bf16[1,192,1536]{2,1,0:T(8,128)(2,1)S(1)}, bf16[1,192,1536]{2,1,0:T(8,128)(2,1)}, u32[]{:S(2)}) copy-start(bf16[1,192,1536]{2,1,0:T(8,128)(2,1)} %wg_ref.7) | copy-start | bytes 1769476
  112.9 16.1 %copy-start.1 = (bf16[1,192,1536]{2,1,0:T(8,128)(2,1)S(1)}, bf16[1,192,1536]{2,1,0:T(8,128)(2,1)}, u32[]{:S(2)}) copy-start(bf16[1,192,1536]{2,1,0:T(8,128)(2,1)} %wu_ref.7) | copy-start | bytes 1769476
  112.9 16.1 %copy-start.2 = (bf16[1,1536,192]{1,2,0:T(8,128)(2,1)S(1)}, bf16[1,1536,192]{1,2,0:T(8,128)(2,1)}, u32[]{:S(2)}) copy-start(bf16[1,1536,192]{1,2,0:T(8,128)(2,1)} %param.17) | copy-start | bytes 1769476
  127.1 4.7 %collective-permute-start.1 = (bf16[128,4608]{1,0:T(8,128)(2,1)S(1)}, bf16[128,4608]{1,0:T(8,128)(2,1)S(1)}, u32[]{:S(2)}, u32[]{:S(2)}) collective-permute-start(bf16[128,4608]{1,0:T(8,128)(2,1)S(1)} %bitcast.9), channel_id=1, source_target_pairs={{0,32},{32,0},{1,33},{33,1},{2,34},{34,2},{3,35},{35,3},{4,36},{36... | collective-permute-start | bytes 3538952 | tf_op jit(solution)/shard_map/ppermute | solution.py:248
  129.8 25.5 %copy-start.3 = (s32[8,2]{0,1:T(2,128)S(1)}, s32[8,2]{0,1:T(2,128)}, u32[]{:S(2)}) copy-start(s32[8,2]{0,1:T(2,128)} %param.11) | copy-start | bytes 196
  129.8 25.5 %copy-start.4 = (f32[8,2]{0,1:T(2,128)S(1)}, f32[8,2]{0,1:T(2,128)}, u32[]{:S(2)}) copy-start(f32[8,2]{0,1:T(2,128)} %param.12) | copy-start | bytes 196

commit v5 on v4

--- a/solution.py
+++ b/solution.py
@@ -106,10 +106,9 @@
     hidden = (gate * sigma * up).astype(LOW)
     gate_grad = (hidden_grad * up * sigma * (1.0 + gate * (1.0 - sigma))).astype(LOW)
     up_grad = (hidden_grad * gate * sigma).astype(LOW)
-    for i in range(copies):
-        out_ref[i, :, :width] = hidden
-        out_ref[i, :, width : 2 * width] = gate_grad
-        out_ref[i, :, 2 * width :] = up_grad
+    out_ref[:, :width] = hidden
+    out_ref[:, width : 2 * width] = gate_grad
+    out_ref[:, 2 * width :] = up_grad
 
 
 def row_products(act_ref, wg_ref, wu_ref, wd_ref):
@@ -241,8 +240,8 @@
     parts = exchange(sums.reshape(n_x, half_rows // n_x, columns), "x")
     sums = jnp.sum(parts.astype(F32), axis=0).astype(LOW)
     parts = exchange(sums.reshape(n_z, sums.shape[0] // n_z, columns), "z_hi")
-    copies = call(middle_kernel, [vmem], vmem, near_out(parts.shape), (near(parts),), LIMIT)
-    act = exchange(copies, "z_hi").reshape(1, half_rows // n_x, columns)
+    act = call(middle_kernel, [vmem], vmem, near_out(parts.shape[1:]), (near(parts),), LIMIT)
+    act = lax.all_gather(act, "z_hi", axis=0, tiled=True)[None]
     act = exchange(jnp.broadcast_to(act, (n_x,) + act.shape[1:]), "x")
     own = act.reshape(half_rows, columns)
     other = lax.ppermute(own, "core", swap)

time: 157 us -> 150 us (0.955)
  blocking collectives: 139 us -> 132 us
    all_to_all x6 -> x5, blocking collectives: 139 us -> 110 us  [exchange(): return lax.all_to_all(value, axis, split_axis=0, concat_axis=0, tiled=True)]
    all_gather x0 -> x1, blocking collectives: none -> 21.7 us  [per_device(): act = lax.all_gather(act, 'z_hi', axis=0, tiled=True)[None]]
where the time goes in v5:
time: 150 us; the launch traced here: 149 us
  blocking collectives  132 us (88%)
  Pallas kernels  9.23 us (6%)
  starting transfers between devices  3.83 us (3%)
  waiting for transfers between devices  2.84 us (2%)
    all_to_all x5, blocking collectives, exchange(): return lax.all_to_all(value, axis, split_axis=0, concat_axis=0, tiled=True)  110 us
    all_gather x1, blocking collectives, per_device(): act = lax.all_gather(act, 'z_hi', axis=0, tiled=True)[None]  21.7 us
    pallas_call x7, Pallas kernels, call(): pl.pallas_call(kernel, out_shape=shapes, in_specs=in_specs, out_specs=out...  9.23 us
  transfers between devices with their start and end apart: 2, of which 2 were waited for; matrix products, arithmetic and copies ran while one was open for 0% of the time, Pallas kernels for 2%

profile of v5, /device:TPU:8, one launch (start us, length us, event | category | flops | bytes accessed | tf_op | source)
XLA Modules:
  0.0 149.3 jit_solution(15191396612035872681)
XLA Ops:
  0.6 0.9 shard_map.128
  1.5 25.9 %all_to_all.25.got_ref = bf16[32,8,384]{2,1,0:T(8,128)(2,1)S(1)} all-to-all(bf16[32,8,384]{2,1,0:T(8,128)(2,1)S(1)} %shard_map.128), channel_id=1, replica_groups=mesh['x'=4,'z_hi'=4,'core'=2,'z_lo'=4,'y'=8] {'z_lo','y'}, dimensions={0} | all-to-all | bytes 393216 | tf_op jit(solution)/shard_map/all_to_all | solution.py:189
  27.4 1.9 %shard_map.130 = bf16[128,4608]{1,0:T(8,128)(2,1)S(1)} custom-call(s32[1]{0:T(128)S(6)} %sub.3.half_ref, bf16[32,8,384]{2,1,0:T(8,128)(2,1)S(1)} %all_to_all.25.got_ref, bf16[1,192,1536]{2,1,0:T(8,128)(2,1)} %wg_ref.7, bf16[1,192,1536]{2,1,0:T(8,128)(2,1)} %wu_ref.7, bf16[1,192,1536]{2,1,0:T(8,128)(2,1)} %bitcast.11), custom_call_target="tpu_custom_call" | custom-call | tf_op jit(solution)/shard_map/pallas_call | solution.py:177
  29.4 1.9 %collective-permute-start = (bf16[128,4608]{1,0:T(8,128)(2,1)S(1)}, bf16[128,4608]{1,0:T(8,128)(2,1)S(1)}, u32[]{:S(2)}, u32[]{:S(2)}) collective-permute-start(bf16[128,4608]{1,0:T(8,128)(2,1)S(1)} %shard_map.130), channel_id=1, source_target_pairs={{0,32},{32,0},{1,33},{33,1},{2,34},{34,2},{3,35},{35,3},{4,36},{36... | collective-permute-start | bytes 3538952 | tf_op jit(solution)/shard_map/ppermute | solution.py:238
  31.3 1.9 %shard_map.129 = bf16[128,4608]{1,0:T(8,128)(2,1)S(1)} custom-call(s32[1]{0:T(128)} %bitcast.2.half_ref, bf16[32,8,384]{2,1,0:T(8,128)(2,1)S(1)} %all_to_all.25.got_ref, bf16[1,192,1536]{2,1,0:T(8,128)(2,1)} %wg_ref.7, bf16[1,192,1536]{2,1,0:T(8,128)(2,1)} %wu_ref.7, bf16[1,192,1536]{2,1,0:T(8,128)(2,1)} %bitcast.12), custom_call_target="tpu_custom_call" | custom-call | tf_op jit(solution)/shard_map/pallas_call | solution.py:177
  33.2 0.9 collective-permute-done
  34.1 0.3 add_convert_fusion
  34.4 19.5 %all_to_all.26 = bf16[4,32,4608]{2,1,0:T(8,128)(2,1)S(1)} all-to-all(bf16[4,32,4608]{2,1,0:T(8,128)(2,1)S(1)} %bitcast.19), channel_id=1, replica_groups=mesh['x'=4,'z_hi'=4,'core'=2,'z_lo'=4,'y'=8] {'x'}, dimensions={0} | all-to-all | bytes 2359296 | tf_op jit(solution)/shard_map/all_to_all | solution.py:189
  53.9 0.3 reduce_sum.12
  54.2 34.9 %all_to_all.27.parts_ref = bf16[4,8,4608]{2,1,0:T(8,128)(2,1)S(1)} all-to-all(bf16[4,8,4608]{2,1,0:T(8,128)(2,1)S(1)} %bitcast.20), channel_id=1, replica_groups=mesh['x'=4,'z_hi'=4,'core'=2,'z_lo'=4,'y'=8] {'z_hi'}, dimensions={0} | all-to-all | bytes 589824 | tf_op jit(solution)/shard_map/all_to_all | solution.py:189
  89.1 0.1 shard_map.131
  89.2 21.7 %all_gather.3 = bf16[32,4608]{1,0:T(8,128)(2,1)S(1)} all-gather(bf16[8,4608]{1,0:T(8,128)(2,1)S(1)} %shard_map.131), channel_id=1, replica_groups=mesh['x'=4,'z_hi'=4,'core'=2,'z_lo'=4,'y'=8] {'z_hi'}, dimensions={0}, use_global_device_ids=true | all-gather | bytes 368640 | tf_op jit(solution)/shard_map/all_gather | solution.py:244
  110.9 0.1 broadcast_in_dim.2
  110.9 0.0 copy-start
  111.0 0.0 copy-start.1
  111.0 0.0 copy-start.2
  111.0 14.2 %all_to_all.28 = bf16[4,32,4608]{2,1,0:T(8,128)(2,1)S(1)} all-to-all(bf16[4,32,4608]{2,1,0:T(8,128)(2,1)S(1)} %broadcast_in_dim.2), channel_id=1, replica_groups=mesh['x'=4,'z_hi'=4,'core'=2,'z_lo'=4,'y'=8] {'x'}, dimensions={0} | all-to-all | bytes 2359296 | tf_op jit(solution)/shard_map/all_to_all | solution.py:189
  125.1 1.9 %collective-permute-start.1 = (bf16[128,4608]{1,0:T(8,128)(2,1)S(1)}, bf16[128,4608]{1,0:T(8,128)(2,1)S(1)}, u32[]{:S(2)}, u32[]{:S(2)}) collective-permute-start(bf16[128,4608]{1,0:T(8,128)(2,1)S(1)} %bitcast.8), channel_id=1, source_target_pairs={{0,32},{32,0},{1,33},{33,1},{2,34},{34,2},{3,35},{35,3},{4,36},{36... | collective-permute-start | bytes 3538952 | tf_op jit(solution)/shard_map/ppermute | solution.py:247
  127.1 0.0 copy-done
  127.1 0.0 copy-done.1
  127.1 0.0 copy-done.2
  127.1 0.8 shard_map.132.held_ref
  127.9 0.0 copy-start.3
  127.9 0.0 copy-start.4
  127.9 2.0 %collective-permute-done.1.other_ref = bf16[128,4608]{1,0:T(8,128)(2,1)S(1)} collective-permute-done((bf16[128,4608]{1,0:T(8,128)(2,1)S(1)}, bf16[128,4608]{1,0:T(8,128)(2,1)S(1)}, u32[]{:S(2)}, u32[]{:S(2)}) %collective-permute-start.1) | collective-permute-done | bytes 1179680 | tf_op jit(solution)/shard_map/ppermute | solution.py:247
  129.9 2.3 %shard_map.133 = (bf16[32,8,384]{2,1,0:T(8,128)(2,1)S(1)}, bf16[1,192,1536]{2,1,0:T(8,128)(2,1)}, bf16[1,192,1536]{2,1,0:T(8,128)(2,1)}, bf16[1,192,1536]{2,1,0:T(8,128)(2,1)}) custom-call(s32[1]{0:T(128)} %bitcast.2.half_ref, bf16[128,4608]{1,0:T(8,128)(2,1)S(1)} %bitcast.10, bf16[128,4608]{1,0:T(8,128)(2,1)S(1)} %collective-permute-done.1.other_ref, ...), custom_call_target="tpu_custom_call" | custom-call | tf_op jit(solution)/shard_map/pallas_call | solution.py:177
  132.2 15.8 %all_to_all.29.back_ref = bf16[32,8,384]{2,1,0:T(8,128)(2,1)S(1)} all-to-all(bf16[32,8,384]{2,1,0:T(8,128)(2,1)S(1)} %get-tuple-element.17), channel_id=1, replica_groups=mesh['x'=4,'z_hi'=4,'core'=2,'z_lo'=4,'y'=8] {'z_lo','y'}, dimensions={0} | all-to-all | bytes 393216 | tf_op jit(solution)/shard_map/all_to_all | solution.py:189
  148.0 0.0 copy-done.3
  148.0 0.0 copy-done.4
  148.0 1.3 shard_map.134
Async XLA Ops:
  29.4 4.7 %collective-permute-start = (bf16[128,4608]{1,0:T(8,128)(2,1)S(1)}, bf16[128,4608]{1,0:T(8,128)(2,1)S(1)}, u32[]{:S(2)}, u32[]{:S(2)}) collective-permute-start(bf16[128,4608]{1,0:T(8,128)(2,1)S(1)} %shard_map.130), channel_id=1, source_target_pairs={{0,32},{32,0},{1,33},{33,1},{2,34},{34,2},{3,35},{35,3},{4,36},{36... | collective-permute-start | bytes 3538952 | tf_op jit(solution)/shard_map/ppermute | solution.py:238
  110.9 16.1 %copy-start = (bf16[1,192,1536]{2,1,0:T(8,128)(2,1)S(1)}, bf16[1,192,1536]{2,1,0:T(8,128)(2,1)}, u32[]{:S(2)}) copy-start(bf16[1,192,1536]{2,1,0:T(8,128)(2,1)} %wg_ref.7) | copy-start | bytes 1769476
  111.0 16.1 %copy-start.1 = (bf16[1,192,1536]{2,1,0:T(8,128)(2,1)S(1)}, bf16[1,192,1536]{2,1,0:T(8,128)(2,1)}, u32[]{:S(2)}) copy-start(bf16[1,192,1536]{2,1,0:T(8,128)(2,1)} %wu_ref.7) | copy-start | bytes 1769476
  111.0 16.1 %copy-start.2 = (bf16[1,1536,192]{1,2,0:T(8,128)(2,1)S(1)}, bf16[1,1536,192]{1,2,0:T(8,128)(2,1)}, u32[]{:S(2)}) copy-start(bf16[1,1536,192]{1,2,0:T(8,128)(2,1)} %param.17) | copy-start | bytes 1769476
  125.1 4.7 %collective-permute-start.1 = (bf16[128,4608]{1,0:T(8,128)(2,1)S(1)}, bf16[128,4608]{1,0:T(8,128)(2,1)S(1)}, u32[]{:S(2)}, u32[]{:S(2)}) collective-permute-start(bf16[128,4608]{1,0:T(8,128)(2,1)S(1)} %bitcast.8), channel_id=1, source_target_pairs={{0,32},{32,0},{1,33},{33,1},{2,34},{34,2},{3,35},{35,3},{4,36},{36... | collective-permute-start | bytes 3538952 | tf_op jit(solution)/shard_map/ppermute | solution.py:247
  127.9 20.1 %copy-start.3 = (s32[8,2]{0,1:T(2,128)S(1)}, s32[8,2]{0,1:T(2,128)}, u32[]{:S(2)}) copy-start(s32[8,2]{0,1:T(2,128)} %param.11) | copy-start | bytes 196
  127.9 20.1 %copy-start.4 = (f32[8,2]{0,1:T(2,128)S(1)}, f32[8,2]{0,1:T(2,128)}, u32[]{:S(2)}) copy-start(f32[8,2]{0,1:T(2,128)} %param.12) | copy-start | bytes 196
